TPU v7x, 32 devices: a whole 2x2x4 slice. The times are simulated.
32 devices in a mesh: dp: 16 (over z, y, x), tensor: 2 (over core).
Axes of the slice: x: 2, y: 2, z: 4, core: 2. Of those that a mesh axis runs over, the one named last changes fastest.
Arguments:
- tokens: bfloat16 [32, 1024, 640], P(('dp', 'tensor')), may hold values from -6 to 6
- out_grad: bfloat16 [32, 1024, 640], P(('dp', 'tensor')), may hold values from -6 to 6
- segment_ids: int32 [32, 1024], P('dp'), may hold values from 0 to 7, never falling along the last dimension, each value on 1 to 512 neighbouring positions
- token_live: int32 [32, 1024], P('dp'), may hold values from 0 to 1, as said below
- live_rows: int32 [16], P('dp'), may hold values from 1 to 2, as said below
- targets: int32 [32, 1024], P(('dp', 'tensor')), may hold values from -33 to 32
- predicted: int32 [32, 1024], P(('dp', 'tensor')), may hold values from 0 to 32
- w_qkv: bfloat16 [3, 640, 640], P(None, None, 'tensor'), may hold values from -0.25 to 0.25
- b_qkv: bfloat16 [3, 640], P(None, 'tensor'), may hold values from -3 to 3
- w_out: bfloat16 [640, 640], P('tensor'), may hold values from -1.25 to 1.25
- b_out: bfloat16 [640], replicated, may hold values from -2 to 2
- norm1_gain: bfloat16 [640], replicated, may hold values from 0.099609375 to 1.8984375
- norm1_bias: bfloat16 [640], replicated, may hold values from -2 to 2
- norm2_gain: bfloat16 [640], replicated, may hold values from 0.099609375 to 1.8984375
- norm2_bias: bfloat16 [640], replicated, may hold values from -2 to 2
- w_up: bfloat16 [640, 2560], P(None, 'tensor'), may hold values from -0.25 to 0.25
- b_up: bfloat16 [2560], P('tensor'), may hold values from -3 to 3
- w_down: bfloat16 [2560, 640], P('tensor'), may hold values from -0.125 to 0.125
- b_down: bfloat16 [640], replicated, may hold values from -2 to 2
Outputs:
- out_act: bfloat16 [32, 1024, 640], P(('dp', 'tensor'))
- in_grad: bfloat16 [32, 1024, 640], P(('dp', 'tensor'))
- grad_w_qkv: float32 [3, 640, 640], P(None, None, 'tensor')
- grad_b_qkv: float32 [3, 640], P(None, 'tensor')
- grad_w_out: float32 [640, 640], P('tensor')
- grad_b_out: float32 [640], replicated
- grad_norm1_gain: float32 [640], replicated
- grad_norm1_bias: float32 [640], replicated
- grad_norm2_gain: float32 [640], replicated
- grad_norm2_bias: float32 [640], replicated
- grad_w_up: float32 [640, 2560], P(None, 'tensor')
- grad_b_up: float32 [2560], P('tensor')
- grad_w_down: float32 [2560, 640], P('tensor')
- grad_b_down: float32 [640], replicated
- counts: int32 [3], replicated
- row_correct: int32 [32], P(('dp', 'tensor'))
Inputs may be any that keep to these rules, and one draw needn't show every extreme that they name: `token_live`: each row's live tokens are a prefix of 512 or more positions. `live_rows`: slots below this count in a data index hold proteins; the rest of its 2 slots are padding. Some data index is full in every draw. `segment_ids`: never falling along a row. `targets`: A negative value marks a position that is not masked.
All inputs are finite; a program needn't handle non-finite values.
Results may differ from a plain program's by a relative error of at most 0.012.
The roundings to bfloat16 on the way count: a program that leaves them out, or rounds other values in their place, can miss the bound.
Values may be sent and summed in bfloat16 or wider, within the bound.
No kernel may reach another device: no remote copies, remote signals or barrier semaphores. Data moves between devices by JAX's collectives and lax.ppermute only.
A program may use at most 192 MiB of HBM per device.

v0:
```python
import math

import jax
import jax.numpy as jnp
from jax import lax
from jax.sharding import PartitionSpec as P

HEAD_DIM = 32
QBLOCK = 512


epsilon = 1e-05
masked_fill = -1000000000.0


def norm_forward(values, gain, shift):
    average = jnp.mean(values, axis=-1, keepdims=True)
    centered = values - average
    variance = jnp.mean(centered * centered, axis=-1, keepdims=True)
    return centered * lax.rsqrt(variance + epsilon) * gain + shift


def norm_backward(upstream, values, gain):
    average = jnp.mean(values, axis=-1, keepdims=True)
    centered = values - average
    variance = jnp.mean(centered * centered, axis=-1, keepdims=True)
    inverse = lax.rsqrt(variance + epsilon)
    normed = centered * inverse
    gain_grad = jnp.sum(upstream * normed, axis=(0, 1))
    shift_grad = jnp.sum(upstream, axis=(0, 1))
    inner = upstream * gain
    result = inverse * (
        inner
        - jnp.mean(inner, axis=-1, keepdims=True)
        - normed * jnp.mean(inner * normed, axis=-1, keepdims=True)
    )
    return (result, gain_grad, shift_grad)


def rotary_tables(segments, head_dim):
    length = segments.shape[1]
    places = jnp.arange(length, dtype=jnp.int32)
    earlier = jnp.concatenate([segments[:, :1] - 1, segments[:, :-1]], axis=1)
    starts = jnp.where(segments != earlier, places[None, :], jnp.zeros_like(segments))
    begins = lax.cummax(starts, axis=1)
    offsets = (places[None, :] - begins).astype(jnp.float32)
    half = head_dim // 2
    inverse = jnp.exp(jnp.arange(half, dtype=jnp.float32) * (-2.0 * math.log(10000.0) / head_dim))
    angles = offsets[:, :, None] * inverse[None, None, :]
    angles = jnp.concatenate([angles, angles], axis=-1)
    return (jnp.cos(angles), jnp.sin(angles))


def rotate_half(values):
    shape = values.shape
    split = values.reshape(shape[:-1] + (shape[-1] // HEAD_DIM, 2, HEAD_DIM // 2))
    turned = jnp.stack([-split[..., 1, :], split[..., 0, :]], axis=-2)
    return turned.reshape(shape)


def rotate_back(values):
    shape = values.shape
    split = values.reshape(shape[:-1] + (shape[-1] // HEAD_DIM, 2, HEAD_DIM // 2))
    turned = jnp.stack([split[..., 1, :], -split[..., 0, :]], axis=-2)
    return turned.reshape(shape)


def gelu_parts(pre):
    normal_cdf = 0.5 * (1.0 + jax.scipy.special.erf(pre * (1.0 / math.sqrt(2.0))))
    slope = normal_cdf + pre * jnp.exp(-0.5 * pre * pre) * (1.0 / math.sqrt(2.0 * math.pi))
    return (pre * normal_cdf, slope)


def block_mask(segments, alive_row, places, begin):
    block_seg = segments[begin : begin + QBLOCK]
    same = (block_seg[:, None] == segments[None, :]) & (alive_row[None, :] > 0)
    diagonal = places[begin : begin + QBLOCK][:, None] == places[None, :]
    return same | diagonal


def split_heads(values):
    length = values.shape[0]
    return values.reshape(length, values.shape[1] // HEAD_DIM, HEAD_DIM)


def attend_forward(pieces):
    query_row, key_row, value_row, segments, alive_row = pieces
    length = query_row.shape[0]
    query_heads = split_heads(query_row)
    key_heads = split_heads(key_row)
    value_heads = split_heads(value_row)
    places = jnp.arange(length, dtype=jnp.int32)
    outputs = []
    logsums = []
    for begin in range(0, length, QBLOCK):
        allowed = block_mask(segments, alive_row, places, begin)
        scores = jnp.einsum(
            "qhe,khe->hqk",
            query_heads[begin : begin + QBLOCK],
            key_heads,
            preferred_element_type=jnp.float32,
        )
        scores = jnp.where(allowed[None], scores, masked_fill)
        highest = jnp.max(scores, axis=-1, keepdims=True)
        powers = jnp.exp(scores - highest)
        denominator = jnp.sum(powers, axis=-1, keepdims=True)
        weights = (powers / denominator).astype(jnp.bfloat16)
        outputs.append(
            jnp.einsum("hqk,khe->qhe", weights, value_heads, preferred_element_type=jnp.float32)
        )
        logsums.append((highest + jnp.log(denominator))[..., 0])
    attended = jnp.concatenate(outputs, axis=0)
    return (attended.reshape(length, query_row.shape[1]), jnp.concatenate(logsums, axis=1))


def attend_backward(pieces):
    query_row, key_row, value_row, grad_row, logsum_row, segments, alive_row = pieces
    length = query_row.shape[0]
    query_heads = split_heads(query_row)
    key_heads = split_heads(key_row)
    value_heads = split_heads(value_row)
    grad_heads = split_heads(grad_row)
    places = jnp.arange(length, dtype=jnp.int32)
    key_grad = jnp.zeros(key_heads.shape, jnp.float32)
    value_grad = jnp.zeros(value_heads.shape, jnp.float32)
    query_grads = []
    for begin in range(0, length, QBLOCK):
        allowed = block_mask(segments, alive_row, places, begin)
        block_query = query_heads[begin : begin + QBLOCK]
        block_grad = grad_heads[begin : begin + QBLOCK]
        scores = jnp.einsum(
            "qhe,khe->hqk", block_query, key_heads, preferred_element_type=jnp.float32
        )
        scores = jnp.where(allowed[None], scores, masked_fill)
        probs = jnp.exp(scores - logsum_row[:, begin : begin + QBLOCK, None])
        prob_grad = jnp.einsum(
            "qhe,khe->hqk", block_grad, value_heads, preferred_element_type=jnp.float32
        )
        central = jnp.sum(probs * prob_grad, axis=-1, keepdims=True)
        score_low = (probs * (prob_grad - central)).astype(jnp.bfloat16)
        query_grads.append(
            jnp.einsum("hqk,khe->qhe", score_low, key_heads, preferred_element_type=jnp.float32)
        )
        key_grad = key_grad + jnp.einsum(
            "hqk,qhe->khe", score_low, block_query, preferred_element_type=jnp.float32
        )
        value_grad = value_grad + jnp.einsum(
            "hqk,qhe->khe",
            probs.astype(jnp.bfloat16),
            block_grad,
            preferred_element_type=jnp.float32,
        )
    columns = query_row.shape[1]
    query_grad = jnp.concatenate(query_grads, axis=0).reshape(length, columns)
    return (query_grad, key_grad.reshape(length, columns), value_grad.reshape(length, columns))


def body(
    tokens,
    out_grad,
    segment_ids,
    token_live,
    live_rows,
    targets,
    predicted,
    w_qkv,
    b_qkv,
    w_out,
    b_out,
    norm1_gain,
    norm1_bias,
    norm2_gain,
    norm2_bias,
    w_up,
    b_up,
    w_down,
    b_down,
):
    share = tokens.shape[0]
    rows_all = segment_ids.shape[0]
    member = lax.axis_index("tensor")
    slots = jnp.arange(rows_all, dtype=jnp.int32)
    alive = token_live * (slots < live_rows[0]).astype(jnp.int32)[:, None]
    alive_share = lax.dynamic_slice_in_dim(alive, member * share, share, 0)
    live_weight = alive_share.astype(jnp.float32)
    masked = (targets >= 0) & (alive_share > 0)
    masked_weight = masked.astype(jnp.float32)
    w_qkv_use, b_qkv_use, w_out_use, w_up_use, b_up_use, w_down_use = (
        w_qkv,
        b_qkv,
        w_out,
        w_up,
        b_up,
        w_down,
    )
    gain_one = norm1_gain.astype(jnp.float32)
    shift_one = norm1_bias.astype(jnp.float32)
    gain_two = norm2_gain.astype(jnp.float32)
    shift_two = norm2_bias.astype(jnp.float32)
    inputs = tokens.astype(jnp.float32)
    normed_share = norm_forward(inputs, gain_one, shift_one).astype(jnp.bfloat16)
    normed_full = lax.all_gather(normed_share, "tensor", axis=0, tiled=True)
    projected = jnp.einsum(
        "rld,cde->crle", normed_full, w_qkv_use, preferred_element_type=jnp.float32
    )
    projected = projected + b_qkv_use.astype(jnp.float32)[:, None, None, :]
    heads_dev = w_qkv_use.shape[2] // HEAD_DIM
    cosine, sine = rotary_tables(segment_ids, HEAD_DIM)
    cosine = jnp.tile(cosine, (1, 1, heads_dev))
    sine = jnp.tile(sine, (1, 1, heads_dev))
    scale = 1.0 / math.sqrt(HEAD_DIM)
    queries = ((projected[0] * cosine + rotate_half(projected[0]) * sine) * scale).astype(
        jnp.bfloat16
    )
    rotated_keys = (projected[1] * cosine + rotate_half(projected[1]) * sine).astype(jnp.bfloat16)
    values = projected[2].astype(jnp.bfloat16)
    attended, logsums = lax.map(attend_forward, (queries, rotated_keys, values, segment_ids, alive))
    mixed = attended.astype(jnp.bfloat16)
    picked = mixed
    branch = lax.psum_scatter(
        jnp.einsum("rle,ed->rld", picked, w_out_use, preferred_element_type=jnp.float32),
        "tensor",
        scatter_dimension=0,
        tiled=True,
    )
    middle = inputs + branch + b_out.astype(jnp.float32)
    second_share = norm_forward(middle, gain_two, shift_two).astype(jnp.bfloat16)
    second_full = lax.all_gather(second_share, "tensor", axis=0, tiled=True)
    hidden = jnp.einsum("rld,df->rlf", second_full, w_up_use, preferred_element_type=jnp.float32)
    hidden = hidden + b_up_use.astype(jnp.float32)
    gelu_value, slope = gelu_parts(hidden)
    activated = gelu_value.astype(jnp.bfloat16)
    picked = activated
    feed = lax.psum_scatter(
        jnp.einsum("rlf,fd->rld", picked, w_down_use, preferred_element_type=jnp.float32).astype(
            jnp.bfloat16
        ),
        "tensor",
        scatter_dimension=0,
        tiled=True,
    ).astype(jnp.float32)
    out_act = (middle + feed + b_down.astype(jnp.float32)).astype(jnp.bfloat16)
    top_grad = out_grad.astype(jnp.float32) * masked_weight[:, :, None]
    grad_b_down = jnp.sum(top_grad, axis=(0, 1))
    top_full = lax.all_gather(top_grad.astype(jnp.bfloat16), "tensor", axis=0, tiled=True)
    grad_w_down = jnp.einsum("rlf,rld->fd", activated, top_full, preferred_element_type=jnp.float32)
    act_grad = jnp.einsum("rld,fd->rlf", top_full, w_down_use, preferred_element_type=jnp.float32)
    hidden_grad = act_grad * slope
    up_low = hidden_grad.astype(jnp.bfloat16)
    grad_b_up = jnp.sum(hidden_grad, axis=(0, 1))
    grad_w_up = jnp.einsum("rld,rlf->df", second_full, up_low, preferred_element_type=jnp.float32)
    picked = up_low
    second_grad = lax.psum_scatter(
        jnp.einsum("rlf,df->rld", picked, w_up_use, preferred_element_type=jnp.float32),
        "tensor",
        scatter_dimension=0,
        tiled=True,
    )
    middle_norm, grad_gain_two, grad_shift_two = norm_backward(second_grad, middle, gain_two)
    middle_grad = top_grad + middle_norm
    grad_b_out = jnp.sum(middle_grad, axis=(0, 1))
    branch_full = lax.all_gather(middle_grad.astype(jnp.bfloat16), "tensor", axis=0, tiled=True)
    grad_w_out = jnp.einsum("rle,rld->ed", mixed, branch_full, preferred_element_type=jnp.float32)
    mixed_grad = jnp.einsum(
        "rld,ed->rle", branch_full, w_out_use, preferred_element_type=jnp.float32
    ).astype(jnp.bfloat16)
    query_grad, key_grad, value_grad = lax.map(
        attend_backward, (queries, rotated_keys, values, mixed_grad, logsums, segment_ids, alive)
    )
    query_pre = (query_grad * cosine + rotate_back(query_grad * sine)) * scale
    key_pre = key_grad * cosine + rotate_back(key_grad * sine)
    proj_grad = jnp.stack([query_pre, key_pre, value_grad])
    grad_b_qkv = jnp.sum(proj_grad, axis=(1, 2))
    proj_low = proj_grad.astype(jnp.bfloat16)
    grad_w_qkv = jnp.einsum(
        "rld,crle->cde", normed_full, proj_low, preferred_element_type=jnp.float32
    )
    picked = proj_low
    first_grad = lax.psum_scatter(
        jnp.einsum("crle,cde->rld", picked, w_qkv_use, preferred_element_type=jnp.float32),
        "tensor",
        scatter_dimension=0,
        tiled=True,
    )
    input_norm, grad_gain_one, grad_shift_one = norm_backward(first_grad, inputs, gain_one)
    in_grad = (middle_grad + input_norm).astype(jnp.bfloat16)
    correct = masked & (predicted == targets)
    row_correct = jnp.sum(correct.astype(jnp.int32), axis=1)
    tallies = jnp.stack(
        [jnp.sum(live_weight), jnp.sum(masked_weight), jnp.sum(correct.astype(jnp.float32))]
    )
    shared = lax.psum(
        (
            grad_b_out,
            grad_b_down,
            grad_gain_one,
            grad_shift_one,
            grad_gain_two,
            grad_shift_two,
            tallies,
        ),
        ("dp", "tensor"),
    )
    summed = lax.psum((grad_w_qkv, grad_b_qkv, grad_w_out, grad_w_up, grad_b_up, grad_w_down), "dp")
    summed_w_qkv, summed_b_qkv, summed_w_out, summed_w_up, summed_b_up, summed_w_down = summed
    totals = shared[6]
    factor = lax.axis_size("dp") / totals[1]
    counts = totals.astype(jnp.int32)
    return (
        out_act,
        in_grad,
        summed_w_qkv * factor,
        summed_b_qkv * factor,
        summed_w_out * factor,
        shared[0] * factor,
        shared[2] * factor,
        shared[3] * factor,
        shared[4] * factor,
        shared[5] * factor,
        summed_w_up * factor,
        summed_b_up * factor,
        summed_w_down * factor,
        shared[1] * factor,
        counts,
        row_correct,
    )


def solution(mesh):
    in_specs = (
        P(("dp", "tensor"), None, None),
        P(("dp", "tensor"), None, None),
        P("dp", None),
        P("dp", None),
        P("dp"),
        P(("dp", "tensor"), None),
        P(("dp", "tensor"), None),
        P(None, None, "tensor"),
        P(None, "tensor"),
        P("tensor", None),
        P(),
        P(),
        P(),
        P(),
        P(),
        P(None, "tensor"),
        P("tensor"),
        P("tensor", None),
        P(),
    )
    out_specs = (
        P(("dp", "tensor"), None, None),
        P(("dp", "tensor"), None, None),
        P(None, None, "tensor"),
        P(None, "tensor"),
        P("tensor", None),
        P(),
        P(),
        P(),
        P(),
        P(),
        P(None, "tensor"),
        P("tensor"),
        P("tensor", None),
        P(),
        P(),
        P(("dp", "tensor")),
    )
    return jax.shard_map(body, mesh=mesh, in_specs=in_specs, out_specs=out_specs, check_vma=False)
```

profile of v0, /device:TPU:0, one launch (start us, length us, event | category | flops | bytes accessed | tf_op | source)
XLA Modules:
  0.0 862.6 jit_solution(9547975817888189722)
XLA Ops:
  18.3 9.8 %all-gather.5.cloned.1.call-done = bf16[2,1024,640]{2,1,0:T(8,128)(2,1)} async-done(((bf16[1,1024,640]{2,1,0:T(8,128)(2,1)}), bf16[2,1024,640]{2,1,0:T(8,128)(2,1)}) %all-gather.5.cloned.1.call-update) | async-done | bytes 2621456 | tf_op jit(solution)/shard_map/all_gather | solution.py:202
  28.1 5.0 add_bitcast_fusion
  38.0 111.3 %while.28 = (s32[]{:T(128)}, bf16[2,1024,320]{1,2,0:T(8,128)(2,1)}, f32[2,10,1024]{2,1,0:T(8,128)}, bf16[2,1024,320]{1,2,0:T(8,128)(2,1)S(1)}, s32[2,1024]{1,0:T...) while((s32[]{:T(128)}, bf16[2,1024,320]{1,2,0:T(8,128)(2,1)}, ...), condition=%wide.region_9.10_spmd.clone, body=%wide.region_4.0_spmd.sunk.clone | while | flops 1442055168 | bytes 325175616 | solution.py:217
  41.1 3.2 select_reduce_fusion.7
  44.3 7.0 copy-done.4
  51.3 5.6 fusion.224
  56.9 9.5 %fusion.225 = bf16[512,10,32]{0,2,1:T(8,128)(2,1)S(1)} fusion(bf16[1024,10,32]{0,2,1:T(8,128)(2,1)S(1)} %bitcast.373, f32[10,512,1024]{2,1,0:T(8,128)} %copy-done.4, f32[10,512]{1,0:T(8,128)S(1)} %fusion.224, f32[10,512]{1,0:T(8,128)S(1)} %get-tuple-element.440, pred[512,1024]{1,0:T(8,128)(4,1)S(1)} %get-tuple-element.437), kind=kOutput, calls=%fused_computation.16.clone.1.clone | convolution fusion | flops 356515840 | bytes 22519808 | tf_op jit(solution)/shard_map/while/body/eval_jaxpr/hqk,khe->qhe/dot_general | solution.py:109
  66.4 3.2 select_reduce_fusion.6
  69.6 7.0 copy-done.3
  76.6 5.6 fusion.222
  82.2 9.6 %fusion.223 = bf16[512,10,32]{0,2,1:T(8,128)(2,1)S(1)} fusion(bf16[1024,10,32]{0,2,1:T(8,128)(2,1)S(1)} %bitcast.374, f32[10,512,1024]{2,1,0:T(8,128)} %copy-done.3, f32[10,512]{1,0:T(8,128)S(1)} %fusion.222, f32[10,512]{1,0:T(8,128)S(1)} %get-tuple-element.436, pred[512,1024]{1,0:T(8,128)(4,1)S(1)} %get-tuple-element.432), kind=kOutput, calls=%fused_computation.15.clone.1.clone | convolution fusion | flops 356515840 | bytes 22519808 | tf_op jit(solution)/shard_map/while/body/eval_jaxpr/hqk,khe->qhe/dot_general | solution.py:109
  96.6 3.2 select_reduce_fusion.7
  99.8 7.0 copy-done.4
  106.8 5.6 fusion.224
  112.4 9.5 %fusion.225 = bf16[512,10,32]{0,2,1:T(8,128)(2,1)S(1)} fusion(bf16[1024,10,32]{0,2,1:T(8,128)(2,1)S(1)} %bitcast.373, f32[10,512,1024]{2,1,0:T(8,128)} %copy-done.4, f32[10,512]{1,0:T(8,128)S(1)} %fusion.224, f32[10,512]{1,0:T(8,128)S(1)} %get-tuple-element.440, pred[512,1024]{1,0:T(8,128)(4,1)S(1)} %get-tuple-element.437), kind=kOutput, calls=%fused_computation.16.clone.1.clone | convolution fusion | flops 356515840 | bytes 22519808 | tf_op jit(solution)/shard_map/while/body/eval_jaxpr/hqk,khe->qhe/dot_general | solution.py:109
  121.9 3.2 select_reduce_fusion.6
  125.1 7.0 copy-done.3
  132.1 5.6 fusion.222
  137.7 9.6 %fusion.223 = bf16[512,10,32]{0,2,1:T(8,128)(2,1)S(1)} fusion(bf16[1024,10,32]{0,2,1:T(8,128)(2,1)S(1)} %bitcast.374, f32[10,512,1024]{2,1,0:T(8,128)} %copy-done.3, f32[10,512]{1,0:T(8,128)S(1)} %fusion.222, f32[10,512]{1,0:T(8,128)S(1)} %get-tuple-element.436, pred[512,1024]{1,0:T(8,128)(4,1)S(1)} %get-tuple-element.432), kind=kOutput, calls=%fused_computation.15.clone.1.clone | convolution fusion | flops 356515840 | bytes 22519808 | tf_op jit(solution)/shard_map/while/body/eval_jaxpr/hqk,khe->qhe/dot_general | solution.py:109
  149.4 5.8 fusion.80
  156.0 13.9 %reduce-scatter.5.cloned.1.call-done = f32[1,1024,640]{2,1,0:T(8,128)} async-done(((f32[2,1024,640]{2,1,0:T(8,128)}), f32[1,1024,640]{2,1,0:T(8,128)}) %reduce-scatter.5.cloned.1.call-update) | async-done | bytes 2621456 | tf_op jit(solution)/shard_map/reduce_scatter | solution.py:220
  177.2 10.6 %all-gather.7.cloned.1.call-done = bf16[2,1024,640]{2,1,0:T(8,128)(2,1)} async-done(((bf16[1,1024,640]{2,1,0:T(8,128)(2,1)}), bf16[2,1024,640]{2,1,0:T(8,128)(2,1)}) %all-gather.7.cloned.1.call-update) | async-done | bytes 2621456 | tf_op jit(solution)/shard_map/all_gather | solution.py:228
  187.8 10.3 %multiply_convert_fusion.2 = (bf16[2,1024,1280]{2,1,0:T(8,128)(2,1)}, f32[2,1024,1280]{2,1,0:T(8,128)}) fusion(f32[1280]{0:T(1024)S(1)} %convert_element_type.141, bf16[2,1024,640]{2,1,0:T(8,128)(2,1)} %all-gather.7.cloned.1.call-done, bf16[640,1280]{1,0:T(8,128)(2,1)S(1)} %copy-done), kind=kOutput, calls=%fused_computation.73 | convolution fusion | flops 3371171840 | bytes 19993600 | tf_op jit(solution)/shard_map/rld,df->rlf/dot_general | solution.py:229
  198.1 4.3 all-gather.9.cloned.1.call-done
  202.4 10.6 %fusion.97 = (f32[1280]{0:T(1024)}, bf16[2,1024,1280]{2,1,0:T(8,128)(2,1)S(1)}) fusion(f32[2,1024,1280]{2,1,0:T(8,128)} %get-tuple-element.241, f32[1280]{0:T(1024)S(1)} %convert_element_type.141, bf16[2,1024,640]{2,1,0:T(8,128)(2,1)} %all-gather.9.cloned.1.call-done, bf16[1280,640]{1,0:T(8,128)(2,1)} %param.40), kind=kOutput, calls=%fused_computation.210 | convolution fusion | flops 3386899200 | bytes 19998720 | tf_op jit(solution)/shard_map/rld,fd->rlf/dot_general | solution.py:247
  215.3 6.0 fusion.62
  222.7 8.2 convolution_convert_fusion
  231.7 4.2 reduce-scatter.9.cloned.1.call-done
  235.9 3.7 multiply_reduce_fusion.2
  239.6 10.4 %reduce-scatter.7.cloned.1.call-done = bf16[1,1024,640]{2,1,0:T(8,128)(2,1)} async-done(((bf16[2,1024,640]{2,1,0:T(8,128)(2,1)}), bf16[1,1024,640]{2,1,0:T(8,128)(2,1)}) %reduce-scatter.7.cloned.1.call-update) | async-done | bytes 1310736 | tf_op jit(solution)/shard_map/reduce_scatter | solution.py:234
  250.0 5.0 fusion.90
  257.8 12.7 %all-gather.11.cloned.1.call-done = bf16[2,1024,640]{2,1,0:T(8,128)(2,1)} async-done(((bf16[1,1024,640]{2,1,0:T(8,128)(2,1)}), bf16[2,1024,640]{2,1,0:T(8,128)(2,1)}) %all-gather.11.cloned.1.call-update) | async-done | bytes 2621456 | tf_op jit(solution)/shard_map/all_gather | solution.py:262
  270.5 4.1 convolution_convert_fusion.1
  274.6 224.6 %while.29 = (s32[]{:T(128)}, f32[2,1024,320]{1,2,0:T(8,128)}, f32[2,1024,320]{1,2,0:T(8,128)}, f32[2,1024,320]{1,2,0:T(8,128)}, bf16[2,1024,320]{1,2,0:T(8,128)(...) while((s32[]{:T(128)}, f32[2,1024,320]{1,2,0:T(8,128)}, ...), condition=%wide.region_20.21_spmd.clone, body=%wide.region_17.20_spmd.sunk.clone | while | flops 3486440448 | bytes 488270208 | solution.py:267
  279.6 8.6 fusion.250
  291.1 7.0 copy-done.2
  298.1 4.5 fusion.252
  302.6 9.5 %fusion.253 = f32[10,32,1024]{2,1,0:T(8,128)S(1)} fusion(f32[10,32,1024]{2,1,0:T(8,128)S(1)} %fusion.252, bf16[512,10,32]{0,2,1:T(8,128)(2,1)} %bitcast.368, f32[10,512,1024]{2,1,0:T(8,128)} %fusion.250, f32[10,512]{1,0:T(8,128)S(1)} %get-tuple-element.475, pred[512,1024]{1,0:T(8,128)(4,1)S(1)} %get-tuple-element.476), kind=kOutput, calls=%fused_computation.48.clone.1.clone | convolution fusion | flops 351600640 | bytes 24465408 | tf_op jit(solution)/shard_map/while/body/eval_jaxpr/hqk,qhe->khe/dot_general | solution.py:147
  313.3 14.4 %multiply_reduce_fusion.12 = (f32[10,512]{1,0:T(8,128)S(1)}, f32[10,512,1024]{2,1,0:T(8,128)}) fusion(f32[10,512,1024]{2,1,0:T(8,128)} %fusion.250, f32[10,512]{1,0:T(8,128)S(1)} %get-tuple-element.475, pred[512,1024]{1,0:T(8,128)(4,1)S(1)} %get-tuple-element.476, bf16[512,10,32]{0,2,1:T(8,128)(2,1)S(1)} %bitcast.369, ...), kind=kOutput, calls=%fused_computation.35.clone.1.clone | convolution fusion | flops 356510720 | bytes 43491328 | tf_op jit(solution)/shard_map/while/body/eval_jaxpr/qhe,khe->hqk/dot_general | solution.py:136
  327.7 14.3 %multiply_convert_fusion.8 = bf16[10,512,1024]{2,1,0:T(8,128)(2,1)S(1)} fusion(f32[10,512,1024]{2,1,0:T(8,128)} %get-tuple-element.478, f32[10,512,1024]{2,1,0:T(8,128)} %fusion.250, f32[10,512]{1,0:T(8,128)S(1)} %get-tuple-element.479, f32[10,512]{1,0:T(8,128)S(1)} %get-tuple-element.475, pred[512,1024]{1,0:T(8,128)(4,1)S(1)} %get-tuple-element.476), kind=kLoop, calls=%fused_computation.34.clone.1.clone | loop fusion | flops 26214400 | bytes 52994048 | tf_op jit(solution)/shard_map/while/body/eval_jaxpr/convert_element_type | solution.py:140
  342.1 3.2 convolution_bitcast_fusion.11
  347.3 14.4 %multiply_reduce_fusion.11 = (f32[10,512]{1,0:T(8,128)S(1)}, f32[10,512,1024]{2,1,0:T(8,128)}) fusion(f32[10,512,1024]{2,1,0:T(8,128)} %copy-done.2, f32[10,512]{1,0:T(8,128)S(1)} %get-tuple-element.466, pred[512,1024]{1,0:T(8,128)(4,1)S(1)} %get-tuple-element.469, bf16[512,10,32]{0,2,1:T(8,128)(2,1)S(1)} %bitcast.367, ...), kind=kOutput, calls=%fused_computation.32.clone.1.clone | convolution fusion | flops 356510720 | bytes 43491328 | tf_op jit(solution)/shard_map/while/body/eval_jaxpr/qhe,khe->hqk/dot_general | solution.py:136
  361.7 14.3 %multiply_convert_fusion.7 = bf16[10,512,1024]{2,1,0:T(8,128)(2,1)S(1)} fusion(f32[10,512,1024]{2,1,0:T(8,128)} %get-tuple-element.472, f32[10,512,1024]{2,1,0:T(8,128)} %copy-done.2, f32[10,512]{1,0:T(8,128)S(1)} %get-tuple-element.473, f32[10,512]{1,0:T(8,128)S(1)} %get-tuple-element.466, pred[512,1024]{1,0:T(8,128)(4,1)S(1)} %get-tuple-element.469), kind=kLoop, calls=%fused_computation.31.clone.1.clone | loop fusion | flops 26214400 | bytes 52994048 | tf_op jit(solution)/shard_map/while/body/eval_jaxpr/convert_element_type | solution.py:140
  378.0 3.3 convolution_bitcast_fusion.10
  391.6 8.6 fusion.250
  403.1 7.0 copy-done.2
  410.1 4.5 fusion.252
  414.6 9.5 %fusion.253 = f32[10,32,1024]{2,1,0:T(8,128)S(1)} fusion(f32[10,32,1024]{2,1,0:T(8,128)S(1)} %fusion.252, bf16[512,10,32]{0,2,1:T(8,128)(2,1)} %bitcast.368, f32[10,512,1024]{2,1,0:T(8,128)} %fusion.250, f32[10,512]{1,0:T(8,128)S(1)} %get-tuple-element.475, pred[512,1024]{1,0:T(8,128)(4,1)S(1)} %get-tuple-element.476), kind=kOutput, calls=%fused_computation.48.clone.1.clone | convolution fusion | flops 351600640 | bytes 24465408 | tf_op jit(solution)/shard_map/while/body/eval_jaxpr/hqk,qhe->khe/dot_general | solution.py:147
  425.4 14.4 %multiply_reduce_fusion.12 = (f32[10,512]{1,0:T(8,128)S(1)}, f32[10,512,1024]{2,1,0:T(8,128)}) fusion(f32[10,512,1024]{2,1,0:T(8,128)} %fusion.250, f32[10,512]{1,0:T(8,128)S(1)} %get-tuple-element.475, pred[512,1024]{1,0:T(8,128)(4,1)S(1)} %get-tuple-element.476, bf16[512,10,32]{0,2,1:T(8,128)(2,1)S(1)} %bitcast.369, ...), kind=kOutput, calls=%fused_computation.35.clone.1.clone | convolution fusion | flops 356510720 | bytes 43491328 | tf_op jit(solution)/shard_map/while/body/eval_jaxpr/qhe,khe->hqk/dot_general | solution.py:136
  439.7 14.3 %multiply_convert_fusion.8 = bf16[10,512,1024]{2,1,0:T(8,128)(2,1)S(1)} fusion(f32[10,512,1024]{2,1,0:T(8,128)} %get-tuple-element.478, f32[10,512,1024]{2,1,0:T(8,128)} %fusion.250, f32[10,512]{1,0:T(8,128)S(1)} %get-tuple-element.479, f32[10,512]{1,0:T(8,128)S(1)} %get-tuple-element.475, pred[512,1024]{1,0:T(8,128)(4,1)S(1)} %get-tuple-element.476), kind=kLoop, calls=%fused_computation.34.clone.1.clone | loop fusion | flops 26214400 | bytes 52994048 | tf_op jit(solution)/shard_map/while/body/eval_jaxpr/convert_element_type | solution.py:140
  454.1 3.2 convolution_bitcast_fusion.11
  459.3 14.4 %multiply_reduce_fusion.11 = (f32[10,512]{1,0:T(8,128)S(1)}, f32[10,512,1024]{2,1,0:T(8,128)}) fusion(f32[10,512,1024]{2,1,0:T(8,128)} %copy-done.2, f32[10,512]{1,0:T(8,128)S(1)} %get-tuple-element.466, pred[512,1024]{1,0:T(8,128)(4,1)S(1)} %get-tuple-element.469, bf16[512,10,32]{0,2,1:T(8,128)(2,1)S(1)} %bitcast.367, ...), kind=kOutput, calls=%fused_computation.32.clone.1.clone | convolution fusion | flops 356510720 | bytes 43491328 | tf_op jit(solution)/shard_map/while/body/eval_jaxpr/qhe,khe->hqk/dot_general | solution.py:136
  473.7 14.3 %multiply_convert_fusion.7 = bf16[10,512,1024]{2,1,0:T(8,128)(2,1)S(1)} fusion(f32[10,512,1024]{2,1,0:T(8,128)} %get-tuple-element.472, f32[10,512,1024]{2,1,0:T(8,128)} %copy-done.2, f32[10,512]{1,0:T(8,128)S(1)} %get-tuple-element.473, f32[10,512]{1,0:T(8,128)S(1)} %get-tuple-element.466, pred[512,1024]{1,0:T(8,128)(4,1)S(1)} %get-tuple-element.469), kind=kLoop, calls=%fused_computation.31.clone.1.clone | loop fusion | flops 26214400 | bytes 52994048 | tf_op jit(solution)/shard_map/while/body/eval_jaxpr/convert_element_type | solution.py:140
  490.0 3.3 convolution_bitcast_fusion.10
  499.2 3.3 bitcast_multiply_fusion.1
  510.2 7.8 convolution_bitcast_fusion.4
  518.2 8.8 %convolution_bitcast_fusion.3 = f32[640,1280]{1,0:T(8,128)} fusion(bf16[2,1024,640]{2,1,0:T(8,128)(2,1)} %all-gather.7.cloned.1.call-done, bf16[2,1024,1280]{2,1,0:T(8,128)(2,1)} %copy-done.71), kind=kOutput, calls=%fused_computation.91 | convolution fusion | flops 3355443200 | bytes 11141120 | tf_op jit(solution)/shard_map/rld,rlf->df/dot_general | solution.py:251
  526.9 10.0 %convolution_bitcast_fusion.2 = f32[1280,640]{1,0:T(8,128)} fusion(bf16[2,1024,1280]{2,1,0:T(8,128)(2,1)} %get-tuple-element.240, bf16[2,1024,640]{2,1,0:T(8,128)(2,1)S(1)} %copy-done.66), kind=kOutput, calls=%fused_computation.90 | convolution fusion | flops 3355443200 | bytes 11141120 | tf_op jit(solution)/shard_map/rlf,rld->fd/dot_general | solution.py:246
  539.7 6.4 fusion.68
  549.6 3.7 fusion.31
  553.3 82.1 %all-reduce.1 = (f32[3,320]{1,0:T(4,128)S(1)}, f32[1280]{0:T(1024)S(1)}) all-reduce(f32[3,320]{1,0:T(4,128)S(1)} %fusion.31, f32[1280]{0:T(1024)S(1)} %copy-done.57), channel_id=1, replica_groups=mesh['dp'=16,'tensor'=2] {'dp'}, use_global_device_ids=true, to_apply=%region_30.31 | all-reduce | flops 2240 | bytes 17920 | tf_op jit(solution)/shard_map/psum | solution.py:304
  638.2 39.2 %all-reduce = (f32[3]{0:T(128)S(1)}, f32[640]{0:T(1024)S(1)}, f32[640]{0:T(1024)S(1)}, f32[640]{0:T(1024)S(1)}, f32[640]{0:T(1024)S(1)}, /*index=5*/f32[640]{0:T(1024)S(1)}, f32[640]{0:T(1024)S(1)}) all-reduce(f32[3]{0:T(128)S(1)} %pad_maximum_fusion.8, f32[640]{0:T(1024)S(1)} %copy-done.49, ...), channel_id=1, replica_groups=mesh['dp'=16,'tensor'=2] {'dp','tensor'}, use_global_device_ids=true, to_apply=%region_28.29 | all-reduce | flops 3843 | bytes 30744 | tf_op jit(solution)/shard_map/psum | solution.py:292
  679.2 161.4 %all-reduce.5.cloned.1.call-done = (f32[3,640,320]{1,2,0:T(8,128)}, f32[320,640]{1,0:T(8,128)}, f32[640,1280]{1,0:T(8,128)}, f32[1280,640]{1,0:T(8,128)}) async-done(((f32[3,640,320]{1,2,0:T(8,128)}, f32[320,640]{1,0:T(8,128)}, f32[640,1280]{1,0:T(8,128)}, f32[1280,640]{1,0:T(8,128)}), (f32[3,640,320]{1,2,0:T(8,128)}, f32[320,640]{1,0:T(8,128)}, f32[640,1280]{1,0:T(8,128)}, ...) | async-done | bytes 9830416 | tf_op jit(solution)/shard_map/psum | solution.py:304
  840.6 4.0 broadcast_multiply_fusion
  (329 shorter events, 105.4 us)
Async XLA Ops:
  7.2 180.6 %copy-start = (bf16[640,1280]{1,0:T(8,128)(2,1)S(1)}, bf16[640,1280]{1,0:T(8,128)(2,1)}, u32[]{:S(2)}) copy-start(bf16[640,1280]{1,0:T(8,128)(2,1)} %param.38) | copy-start | bytes 4915204
  7.2 5.1 copy-start.7
  7.2 20.9 %all-gather.5.cloned.1.call-start = ((), (), s32[]{:S(2)}) async-start(), calls=%async_computation.4 | async-start | bytes 3932160 | tf_op jit(solution)/shard_map/all_gather | solution.py:202
  8.1 5.8 copy-start.43
  10.3 3.6 copy-start.41
  10.4 4.4 copy-start.60
  10.4 4.4 copy-start.36
  12.3 3.7 copy-start.45
  12.3 6.0 copy-start.58
  13.9 14.2 %copy-start.69 = (bf16[3,640,320]{1,2,0:T(8,128)(2,1)S(1)}, bf16[3,640,320]{1,2,0:T(8,128)(2,1)}, u32[]{:S(2)}) copy-start(bf16[3,640,320]{1,2,0:T(8,128)(2,1)} %param.30) | copy-start | bytes 3686404
  13.9 155.9 %reduce-scatter.5.cloned.1.call-start = ((), (), s32[]{:S(2)}) async-start(), calls=%async_computation.5 | async-start | bytes 7864320 | tf_op jit(solution)/shard_map/reduce_scatter | solution.py:220
  17.0 17.9 %copy-start.33 = (f32[2,1024,32]{1,2,0:T(8,128)}, f32[2,1024,32]{1,2,0:T(8,128)S(1)}, u32[]{:S(2)}) copy-start(f32[2,1024,32]{1,2,0:T(8,128)S(1)} %get-tuple-element.238) | copy-start | bytes 786436
  17.0 17.9 %copy-start.35 = (f32[2,1024,32]{1,2,0:T(8,128)}, f32[2,1024,32]{1,2,0:T(8,128)S(1)}, u32[]{:S(2)}) copy-start(f32[2,1024,32]{1,2,0:T(8,128)S(1)} %get-tuple-element.239) | copy-start | bytes 786436
  38.0 111.4 %copy-start.40 = (bf16[320,640]{1,0:T(8,128)(2,1)S(1)}, bf16[320,640]{1,0:T(8,128)(2,1)}, u32[]{:S(2)}) copy-start(bf16[320,640]{1,0:T(8,128)(2,1)} %param.32) | copy-start | bytes 1228804
  38.2 2.8 copy-start.12
  44.3 7.0 copy-start.4
  69.6 7.0 copy-start.3
  82.2 9.7 %copy-start.38 = (f32[2,10,1024]{2,1,0:T(8,128)S(1)}, f32[2,10,1024]{2,1,0:T(8,128)}, u32[]{:S(2)}) copy-start(f32[2,10,1024]{2,1,0:T(8,128)} %get-tuple-element.504) | copy-start | bytes 245764 | tf_op jit(solution)/shard_map/while
  82.2 9.7 %copy-start.27 = (bf16[2,1024,320]{1,2,0:T(8,128)(2,1)S(1)}, bf16[2,1024,320]{1,2,0:T(8,128)(2,1)}, u32[]{:S(2)}) copy-start(bf16[2,1024,320]{1,2,0:T(8,128)(2,1)} %get-tuple-element.503) | copy-start | bytes 3932164 | tf_op jit(solution)/shard_map/while
  93.7 2.7 copy-start.12
  99.8 7.0 copy-start.4
  125.1 7.0 copy-start.3
  137.7 9.7 %copy-start.38 = (f32[2,10,1024]{2,1,0:T(8,128)S(1)}, f32[2,10,1024]{2,1,0:T(8,128)}, u32[]{:S(2)}) copy-start(f32[2,10,1024]{2,1,0:T(8,128)} %get-tuple-element.504) | copy-start | bytes 245764 | tf_op jit(solution)/shard_map/while
  137.7 9.7 %copy-start.27 = (bf16[2,1024,320]{1,2,0:T(8,128)(2,1)S(1)}, bf16[2,1024,320]{1,2,0:T(8,128)(2,1)}, u32[]{:S(2)}) copy-start(bf16[2,1024,320]{1,2,0:T(8,128)(2,1)} %get-tuple-element.503) | copy-start | bytes 3932164 | tf_op jit(solution)/shard_map/while
  149.4 5.9 copy-start.10
  155.2 14.6 %copy-start.8 = (bf16[1,1024,640]{2,1,0:T(8,128)(2,1)S(1)}, bf16[1,1024,640]{2,1,0:T(8,128)(2,1)}, u32[]{:S(2)}) copy-start(bf16[1,1024,640]{2,1,0:T(8,128)(2,1)} %param.23) | copy-start | bytes 3932164
  155.3 32.5 %all-gather.7.cloned.1.call-start = ((), (), s32[]{:S(2)}) async-start(), calls=%async_computation.6 | async-start | bytes 3932160 | tf_op jit(solution)/shard_map/all_gather | solution.py:228
  173.5 2.3 copy-start.30
  175.0 27.3 %all-gather.9.cloned.1.call-start = ((), (), s32[]{:S(2)}) async-start(), calls=%async_computation.8 | async-start | bytes 3932160 | tf_op jit(solution)/shard_map/all_gather | solution.py:245
  175.8 22.3 %copy-start.47 = (pred[1,1024]{1,0:T(4,128)(4,1)}, pred[1,1024]{1,0:T(4,128)(4,1)S(1)}, u32[]{:S(2)}) copy-start(pred[1,1024]{1,0:T(4,128)(4,1)S(1)} %get-tuple-element.185) | copy-start | bytes 3076
  177.1 58.7 %reduce-scatter.9.cloned.1.call-start = ((), (), s32[]{:S(2)}) async-start(), calls=%async_computation.9 | async-start | bytes 7864320 | tf_op jit(solution)/shard_map/reduce_scatter | solution.py:253
  213.0 2.4 copy-start.71
  221.3 28.7 %reduce-scatter.7.cloned.1.call-start = ((), (), s32[]{:S(2)}) async-start(), calls=%async_computation.7 | async-start | bytes 3932160 | tf_op jit(solution)/shard_map/reduce_scatter | solution.py:234
  231.0 39.5 %all-gather.11.cloned.1.call-start = ((), (), s32[]{:S(2)}) async-start(), calls=%async_computation.10 | async-start | bytes 3932160 | tf_op jit(solution)/shard_map/all_gather | solution.py:262
  257.7 377.6 %reduce-scatter.11.cloned.1.call-start = ((), (), s32[]{:S(2)}) async-start(), calls=%async_computation.11 | async-start | bytes 7864320 | tf_op jit(solution)/shard_map/reduce_scatter | solution.py:279
  274.8 4.7 copy-start.11
  274.8 4.7 copy-start.13
  291.1 7.0 copy-start.2
  381.3 2.5 copy-start.24
  386.8 4.7 copy-start.11
  386.8 4.7 copy-start.13
  403.1 7.0 copy-start.2
  493.3 2.5 copy-start.24
  503.5 2.5 copy-start.26
  506.0 4.1 copy-start.70
  517.9 322.7 %all-reduce.5.cloned.1.call-start = ((), (), s32[]{:S(2)}) async-start(), calls=%async_computation.12 | async-start | bytes 19660800 | tf_op jit(solution)/shard_map/psum | solution.py:304
  518.1 8.8 %copy-start.66 = (bf16[2,1024,640]{2,1,0:T(8,128)(2,1)S(1)}, bf16[2,1024,640]{2,1,0:T(8,128)(2,1)}, u32[]{:S(2)}) copy-start(bf16[2,1024,640]{2,1,0:T(8,128)(2,1)} %all-gather.9.cloned.1.call-done) | copy-start | bytes 7864324
  526.9 10.0 %copy-start.29 = (bf16[2,1024,320]{1,2,0:T(8,128)(2,1)S(1)}, bf16[2,1024,320]{1,2,0:T(8,128)(2,1)}, u32[]{:S(2)}) copy-start(bf16[2,1024,320]{1,2,0:T(8,128)(2,1)} %get-tuple-element.118) | copy-start | bytes 3932164
  526.9 10.0 %copy-start.67 = (bf16[2,1024,640]{2,1,0:T(8,128)(2,1)S(1)}, bf16[2,1024,640]{2,1,0:T(8,128)(2,1)}, u32[]{:S(2)}) copy-start(bf16[2,1024,640]{2,1,0:T(8,128)(2,1)} %all-gather.11.cloned.1.call-done) | copy-start | bytes 7864324
  526.9 12.1 %copy-start.65 = (bf16[2,1024,640]{2,1,0:T(8,128)(2,1)S(1)}, bf16[2,1024,640]{2,1,0:T(8,128)(2,1)}, u32[]{:S(2)}) copy-start(bf16[2,1024,640]{2,1,0:T(8,128)(2,1)} %all-gather.5.cloned.1.call-done) | copy-start | bytes 7864324
  536.9 2.8 copy-start.20
  549.5 3.7 copy-start.57
  549.5 85.8 %copy-start.9 = (bf16[1,1024,640]{2,1,0:T(8,128)(2,1)S(1)}, bf16[1,1024,640]{2,1,0:T(8,128)(2,1)}, u32[]{:S(2)}) copy-start(bf16[1,1024,640]{2,1,0:T(8,128)(2,1)} %param.23) | copy-start | bytes 3932164
  549.5 85.8 %copy-start.42 = (f32[1024]{0:T(1024)S(1)}, f32[1024]{0:T(1024)}, u32[]{:S(2)}) copy-start(f32[1024]{0:T(1024)} %copy-done.41) | copy-start | bytes 12292
  549.5 85.8 %copy-start.44 = (f32[640]{0:T(1024)S(1)}, f32[640]{0:T(1024)}, u32[]{:S(2)}) copy-start(f32[640]{0:T(1024)} %copy-done.43) | copy-start | bytes 7684
  549.5 85.8 %copy-start.46 = (f32[1024]{0:T(1024)S(1)}, f32[1024]{0:T(1024)}, u32[]{:S(2)}) copy-start(f32[1024]{0:T(1024)} %copy-done.45) | copy-start | bytes 12292
  553.2 84.9 %copy-start.49 = (f32[640]{0:T(1024)S(1)}, f32[640]{0:T(1024)}, u32[]{:S(2)}) copy-start(f32[640]{0:T(1024)} %get-tuple-element.186) | copy-start | bytes 7684
  553.2 84.9 %copy-start.50 = (f32[640]{0:T(1024)S(1)}, f32[640]{0:T(1024)}, u32[]{:S(2)}) copy-start(f32[640]{0:T(1024)} %get-tuple-element.233) | copy-start | bytes 7684
  553.2 84.9 %copy-start.55 = (f32[640]{0:T(1024)S(1)}, f32[640]{0:T(1024)}, u32[]{:S(2)}) copy-start(f32[640]{0:T(1024)} %get-tuple-element.123) | copy-start | bytes 7684
  553.3 84.9 %copy-start.56 = (f32[640]{0:T(1024)S(1)}, f32[640]{0:T(1024)}, u32[]{:S(2)}) copy-start(f32[640]{0:T(1024)} %get-tuple-element.129) | copy-start | bytes 7684
  840.6 4.6 copy-start.31
  845.2 3.5 copy-start.32
  847.2 6.7 copy-start.16
  848.1 5.8 copy-start.15
  (32 other events, 42.7 us)
Sparse Core Ops, SparseCore 0:
  14.0 14.0 all-gather.4
  155.4 14.3 reduce-scatter.4
  175.2 12.5 all-gather.6
  189.8 12.5 all-gather.8
  221.4 14.3 reduce-scatter.8
  238.5 11.4 reduce-scatter.6
  257.9 12.5 all-gather.10
  518.0 14.3 reduce-scatter.10
  546.3 294.3 all-reduce.4
where the time goes:
time: 869 us; the launch traced here: 863 us
  matrix products  266 us (31%)
  waiting for transfers between devices  227 us (26%)
  other arithmetic  148 us (17%)
  blocking collectives  121 us (14%)
  local copies, waits for them, and re-layouts  82 us (9%)
  between operations  16.2 us (2%)
    psum x1, waiting for transfers between devices, body(): lax.psum((grad_w_qkv, grad_b_qkv, grad_w_out, grad_w_up, grad_b_up, grad_...  161 us
    psum x1, blocking collectives, body(): lax.psum((grad_w_qkv, grad_b_qkv, grad_w_out, grad_w_up, grad_b_up, grad_...  82.1 us
    dot_general x4, matrix products, attend_backward(): jnp.einsum('qhe,khe->hqk', block_grad, value_heads, preferred_element_typ...  57.5 us
    convert_element_type x4, other arithmetic, attend_backward(): score_low = (probs * (prob_grad - central)).astype(jnp.bfloat16)  57.4 us
    while x60, local copies, waits for them, and re-layouts  55.5 us
    psum x1, blocking collectives, body(): lax.psum((grad_b_out, grad_b_down, grad_gain_one, grad_shift_one, grad_ga...  39.2 us
    dot_general x4, matrix products, attend_forward(): jnp.einsum('hqk,khe->qhe', weights, value_heads, preferred_element_type=j...  38.2 us
    dot_general x4, matrix products, attend_backward(): jnp.einsum('hqk,qhe->khe', probs.astype(jnp.bfloat16), block_grad, prefer...  28.1 us
  transfers between devices with their start and end apart: 9, of which 8 were waited for; matrix products, arithmetic and copies ran while one was open for 8% of the time, Pallas kernels for 0%

commit v1 on v0

v1 whole, which is shorter than its diff:
```python
import functools, math
import numpy as np
import jax, jax.numpy as jnp
from jax import lax
from jax.experimental import pallas as pl
from jax.experimental.pallas import tpu as pltpu
from jax.sharding import PartitionSpec as P
BF=jnp.bfloat16; F32=jnp.float32
QB=256; CH=128; TILE=128; HD=32; NEG=-1e9

def nn(a,b): return lax.dot_general(a,b,(((1,),(0,)),((),())),preferred_element_type=F32)
def nt(a,b): return lax.dot_general(a,b,(((1,),(1,)),((),())),preferred_element_type=F32)
def tn(a,b): return lax.dot_general(a,b,(((0,),(0,)),((),())),preferred_element_type=F32)

def seg_start(meta,idx):
    out=jnp.zeros_like(idx)
    for s in range(1,8):
        out=jnp.where(idx>=meta[s],meta[s],out)
    return out

def key_range(meta,first,length,backward):
    live=meta[9]
    lo=jnp.int32(0); hi=jnp.int32(length)
    for s in range(1,8):
        lo=jnp.where(meta[s]<=first,meta[s],lo)
    for s in range(7,0,-1):
        hi=jnp.where(meta[s]>first+QB-1,meta[s],hi)
    if backward:
        hi=jnp.minimum(hi,live)
    else:
        hi=jnp.minimum(hi,jnp.maximum(live,first+QB))
        lo=jnp.where(lo>=live,first,lo)
    k0=lax.div(lo,CH)*CH
    span=jnp.maximum(lax.div(hi+CH-1,CH)*CH-k0,2*CH)
    k0=jnp.minimum(k0,length-span)
    return pl.multiple_of(k0,CH),span

def bias_block(meta,first,k0,w,qn):
    live=meta[9]
    ki=lax.broadcasted_iota(jnp.int32,(w,1),0)+k0
    qi=lax.broadcasted_iota(jnp.int32,(1,qn),1)+first
    ks=jnp.where(ki<live,seg_start(meta,ki),-1)
    qs=seg_start(meta,qi)
    ok=(ks==qs)|(ki==qi)
    return jnp.where(ok,0.0,NEG).astype(F32)

RC=128
def fwd_kernel(meta,q_ref,k_ref,v_ref,o_ref,lse_ref,vt,bias,sbuf,pbuf):
    qb=pl.program_id(1)
    length=k_ref.shape[0]
    first=qb*QB
    @pl.when(qb==0)
    def _():
        vt[...]=v_ref[...].T
    k0,span=key_range(meta,first,length,False)
    lane=lax.broadcasted_iota(jnp.int32,(QB,TILE),1)
    nh=TILE//HD
    for w in range(2*CH,length+1,CH):
        @pl.when(span==w)
        def _(w=w):
            for c in range(0,w,RC):
                bias[c:c+RC,:]=bias_block(meta,first,k0+c,RC,QB)
            q=q_ref[...]
            outs=[]
            def scores(h):
                qm=jnp.where(lax.div(lane,HD)==h,q,jnp.zeros_like(q))
                top=None
                for c in range(0,w,RC):
                    s=nt(k_ref[pl.ds(k0+c,RC),:],qm)+bias[c:c+RC,:]
                    sbuf[h%2,c:c+RC,:]=s
                    t=jnp.max(s.reshape(RC//8,8,QB),axis=0)
                    top=t if top is None else jnp.maximum(top,t)
                return jnp.max(top,axis=0,keepdims=True)
            def rest(h,m):
                tot=None
                for c in range(0,w,RC):
                    e=jnp.exp(sbuf[h%2,c:c+RC,:]-m)
                    t=jnp.sum(e.reshape(RC//8,8,QB),axis=0)
                    tot=t if tot is None else tot+t
                    pbuf[h%2,c:c+RC,:]=e.astype(BF)
                l=jnp.sum(tot,axis=0,keepdims=True)
                o=nn(vt[h*HD:(h+1)*HD,pl.ds(k0,w)],pbuf[h%2,0:w,:])
                outs.append(o/l)
                lse_ref[0,h:h+1,:]=m+jnp.log(l)
            ms=[scores(0)]
            for h in range(nh):
                if h+1<nh: ms.append(scores(h+1))
                rest(h,ms[h])
            o_ref[...]=jnp.concatenate(outs,axis=0).T.astype(BF)

def attend_fwd(meta,q,k,v):
    length,cols=q.shape
    tiles=cols//TILE
    return pl.pallas_call(fwd_kernel,
        out_shape=(jax.ShapeDtypeStruct((length,cols),BF),jax.ShapeDtypeStruct((tiles,TILE//HD,length),F32)),
        grid_spec=pltpu.PrefetchScalarGridSpec(num_scalar_prefetch=1,grid=(tiles,length//QB),
            in_specs=[pl.BlockSpec((QB,TILE),lambda t,b,m:(b,t)),pl.BlockSpec((length,TILE),lambda t,b,m:(0,t)),pl.BlockSpec((length,TILE),lambda t,b,m:(0,t))],
            out_specs=(pl.BlockSpec((QB,TILE),lambda t,b,m:(b,t)),pl.BlockSpec((1,TILE//HD,QB),lambda t,b,m:(t,0,b))),
            scratch_shapes=[pltpu.VMEM((TILE,length),BF),pltpu.VMEM((length,QB),F32),pltpu.VMEM((2,length,QB),F32),pltpu.VMEM((2,length,QB),BF)]),
        compiler_params=pltpu.CompilerParams(vmem_limit_bytes=40<<20),
        cost_estimate=pl.CostEstimate(flops=4*20*32*1024*1024,bytes_accessed=6<<20,transcendentals=0),
        name="attend_fwd")(meta,q,k,v)

def rope_back(x,cos,sin_b):
    y=x*sin_b
    lane=lax.broadcasted_iota(jnp.int32,x.shape,1)
    low=(lane & 16)==0
    return x*cos+jnp.where(low,pltpu.roll(y,TILE-16,1),-pltpu.roll(y,16,1))

def bwd_kernel(meta,q_ref,k_ref,v_ref,o_ref,do_ref,lse_ref,cos_ref,sin_ref,dq_ref,dk_ref,dv_ref,sum_ref,
               kt,bias,pall,dsall,dkacc,dvacc):
    qb=pl.program_id(1); nqb=pl.num_programs(1)
    length=k_ref.shape[0]
    first=pl.multiple_of(qb*QB,QB)
    nh=TILE//HD
    @pl.when(qb==0)
    def _():
        kt[...]=k_ref[...].T
        dkacc[...]=jnp.zeros_like(dkacc)
        dvacc[...]=jnp.zeros_like(dvacc)
        sum_ref[...]=jnp.zeros_like(sum_ref)
        dq_ref[...]=jnp.zeros_like(dq_ref)
    live=meta[9]
    k0,span=key_range(meta,first,length,True)
    lane=lax.broadcasted_iota(jnp.int32,(QB,TILE),1)
    for w in range(2*CH,length+1,CH):
        @pl.when((span==w)&(first<live))
        def _(w=w):
            for c in range(0,w,RC):
                bias[c:c+RC,:]=bias_block(meta,first,k0+c,RC,QB)
            q=q_ref[...]; do=do_ref[...]
            x=do.astype(F32)*o_ref[...].astype(F32)
            hi=x.astype(BF); lo=(x-hi.astype(F32)).astype(BF)
            pick=(lax.div(lax.broadcasted_iota(jnp.int32,(8,TILE),1),HD)==lax.broadcasted_iota(jnp.int32,(8,TILE),0))
            pick=jnp.where(pick,1.0,0.0).astype(BF)
            delta=nt(pick,hi)+nt(pick,lo)
            qms=[];dms=[];dqs=[]
            for h in range(nh):
                mine=lax.div(lane,HD)==h
                qm=jnp.where(mine,q,jnp.zeros_like(q)); dm=jnp.where(mine,do,jnp.zeros_like(do))
                qms.append(qm);dms.append(dm)
                lse_h=lse_ref[0,h:h+1,:]; del_h=delta[h:h+1,:]
                for c in range(0,w,RC):
                    p=jnp.exp(nt(k_ref[pl.ds(k0+c,RC),:],qm)+bias[c:c+RC,:]-lse_h)
                    pall[c:c+RC,h*QB:(h+1)*QB]=p.astype(BF)
                    ds=(p*(nt(v_ref[pl.ds(k0+c,RC),:],dm)-del_h)).astype(BF)
                    dsall[c:c+RC,h*QB:(h+1)*QB]=ds
                dqs.append(nn(kt[h*HD:(h+1)*HD,pl.ds(k0,w)],dsall[0:w,h*QB:(h+1)*QB]))
            dvacc[pl.ds(k0,w),:]+=nn(pall[0:w,:],jnp.concatenate(dms,axis=0))
            dkacc[pl.ds(k0,w),:]+=nn(dsall[0:w,:],jnp.concatenate(qms,axis=0))
            dq=jnp.concatenate(dqs,axis=0).T
            dq=rope_back(dq,cos_ref[pl.ds(first,QB),:],sin_ref[pl.ds(first,QB),:])*(1.0/math.sqrt(HD))
            sum_ref[0,0:1,:]+=jnp.sum(dq,axis=0,keepdims=True)
            dq_ref[pl.ds(first,QB),:]=dq.astype(BF)
    @pl.when(qb==nqb-1)
    def _():
        dk=rope_back(dkacc[...],cos_ref[...],sin_ref[...])
        sum_ref[0,1:2,:]=jnp.sum(dk,axis=0,keepdims=True)
        dk_ref[...]=dk.astype(BF)
        dv=dvacc[...]
        sum_ref[0,2:3,:]=jnp.sum(dv,axis=0,keepdims=True)
        dv_ref[...]=dv.astype(BF)

def attend_bwd(meta,q,k,v,o,do,lse,cos,sin):
    length,cols=q.shape
    tiles=cols//TILE
    blk=pl.BlockSpec((QB,TILE),lambda t,b,m:(b,t)); col=pl.BlockSpec((length,TILE),lambda t,b,m:(0,t)); tab=pl.BlockSpec((length,TILE),lambda t,b,m:(0,0))
    sd=jax.ShapeDtypeStruct
    return pl.pallas_call(bwd_kernel,
        out_shape=(sd((length,cols),BF),)*3+(sd((tiles,8,TILE),F32),),
        grid_spec=pltpu.PrefetchScalarGridSpec(num_scalar_prefetch=1,grid=(tiles,length//QB),
            in_specs=[blk,col,col,blk,blk,pl.BlockSpec((1,TILE//HD,QB),lambda t,b,m:(t,0,b)),tab,tab],
            out_specs=(col,col,col,pl.BlockSpec((1,8,TILE),lambda t,b,m:(t,0,0))),
            scratch_shapes=[pltpu.VMEM((TILE,length),BF),pltpu.VMEM((length,QB),F32),pltpu.VMEM((length,4*QB),BF),pltpu.VMEM((length,4*QB),BF),
                            pltpu.VMEM((length,TILE),F32),pltpu.VMEM((length,TILE),F32)]),
        compiler_params=pltpu.CompilerParams(vmem_limit_bytes=48<<20),
        cost_estimate=pl.CostEstimate(flops=10*20*32*1024*1024,bytes_accessed=10<<20,transcendentals=0),
        name="attend_bwd")(meta,q,k,v,o,do,lse,cos,sin)
EPS=1e-5
TB=256
def ln_stats(x):
    mu=jnp.mean(x,axis=-1,keepdims=True)
    c=x-mu
    var=jnp.mean(c*c,axis=-1,keepdims=True)
    r=lax.rsqrt(var+EPS)
    return c*r,r

def rope_tables(length):
    lane=np.arange(TILE)%(HD//2)
    inv=np.exp(lane.astype(np.float64)*(-2.0*math.log(10000.0)/HD))
    ang=np.arange(length,dtype=np.float64)[:,None]*inv[None,:]
    return np.cos(ang).astype(np.float32),np.sin(ang).astype(np.float32)

def qkv_kernel(meta,x_ref,wo_ref,wp_ref,b_ref,g_ref,s_ref,ct_ref,st_ref,n_ref,q_ref,k_ref,v_ref,cos_ref,sin_ref,wc_ref):
    i=pl.program_id(0)
    half=wo_ref.shape[2]
    @pl.when(i==0)
    def _():
        for c in range(3):
            wc_ref[c]=jnp.concatenate([wo_ref[c],wp_ref[c]],axis=1)
    x=x_ref[...].astype(F32)
    nrm,_=ln_stats(x)
    n=(nrm*g_ref[...].astype(F32)+s_ref[...].astype(F32)).astype(BF)
    n_ref[...]=n
    first=i*TB
    top=ct_ref.shape[0]-1
    j=lax.broadcasted_iota(jnp.int32,(TB,TILE),0)+first
    cc=jnp.broadcast_to(ct_ref[0:1,:],(TB,TILE)); ss=jnp.broadcast_to(st_ref[0:1,:],(TB,TILE))
    for s in range(1,8):
        at=meta[s]; row=jnp.minimum(at,top)
        past=j>=at
        cc=jnp.where(past,ct_ref[pl.ds(row,1),:],cc)
        ss=jnp.where(past,st_ref[pl.ds(row,1),:],ss)
    cj=ct_ref[pl.ds(pl.multiple_of(first,TB),TB),:]; sj=st_ref[pl.ds(pl.multiple_of(first,TB),TB),:]
    cos=cj*cc+sj*ss; sin=sj*cc-cj*ss
    cos_ref[...]=cos; sin_ref[...]=sin
    low=(lax.broadcasted_iota(jnp.int32,(TB,TILE),1)&16)==0
    signed=jnp.where(low,-sin,sin)
    for c,(out,scale) in enumerate(((q_ref,1.0/math.sqrt(HD)),(k_ref,None),(v_ref,None))):
        p=nn(n,wc_ref[c])+b_ref[c:c+1,:]
        if c==2:
            out[...]=p.astype(BF)
        else:
            for t in range(p.shape[1]//TILE):
                y=p[:,t*TILE:(t+1)*TILE]
                z=y*cos+jnp.where(low,pltpu.roll(y,TILE-16,1),pltpu.roll(y,16,1))*signed
                if scale is not None: z=z*scale
                out[:,t*TILE:(t+1)*TILE]=z.astype(BF)

def full(shape):
    return pl.BlockSpec(shape,lambda *a:(0,)*len(shape))
def params(mb): return pltpu.CompilerParams(vmem_limit_bytes=mb<<20)
sd=jax.ShapeDtypeStruct

def qkv_call(meta,x,w_own,w_par,b,g,s):
    T,D=x.shape; half=w_own.shape[2]; inner=2*half
    ct,st=rope_tables(T)
    rows=lambda n:pl.BlockSpec((TB,n),lambda i,m:(i,0))
    return pl.pallas_call(qkv_kernel,
        out_shape=(sd((T,D),BF),sd((T,inner),BF),sd((T,inner),BF),sd((T,inner),BF),sd((T,TILE),F32),sd((T,TILE),F32),sd((3,D,inner),BF)),
        grid_spec=pltpu.PrefetchScalarGridSpec(num_scalar_prefetch=1,grid=(T//TB,),
            in_specs=[rows(D),full(w_own.shape),full(w_par.shape),full((3,inner)),full((1,D)),full((1,D)),full((T,TILE)),full((T,TILE))],
            out_specs=(rows(D),rows(inner),rows(inner),rows(inner),rows(TILE),rows(TILE),full((3,D,inner)))),
        compiler_params=params(44),
        cost_estimate=pl.CostEstimate(flops=2*T*D*3*inner,bytes_accessed=12<<20,transcendentals=0),
        name="norm_qkv_rope")(meta,x,w_own,w_par,b,g,s,jnp.asarray(ct),jnp.asarray(st))

def gelu_parts(h):
    cdf=0.5*(1.0+lax.erf(h*(1.0/math.sqrt(2.0))))
    return h*cdf, cdf+h*jnp.exp(-0.5*h*h)*(1.0/math.sqrt(2.0*math.pi))

FC=256
def ffn_kernel(meta,mix_ref,x_ref,og_ref,tg_ref,woo_ref,wop_ref,bo_ref,g_ref,s_ref,wuo_ref,wup_ref,buo_ref,bup_ref,wdo_ref,wdp_ref,bd_ref,
               n2_ref,dl_ref,ao_ref,ap_ref,uo_ref,up_ref,out_ref,mg_ref,bl_ref,xg_ref,sum_ref,sbo_ref,sbp_ref,wo,feed,sg):
    i=pl.program_id(0)
    @pl.when(i==0)
    def _():
        wo[...]=jnp.concatenate([woo_ref[...],wop_ref[...]],axis=0)
        sum_ref[...]=jnp.zeros_like(sum_ref); sbo_ref[...]=jnp.zeros_like(sbo_ref); sbp_ref[...]=jnp.zeros_like(sbp_ref)
    live=meta[9]
    mid=x_ref[...].astype(F32)+nn(mix_ref[...],wo[...])+bo_ref[...].astype(F32)
    nrm,r=ln_stats(mid)
    g=g_ref[...].astype(F32)
    n2=(nrm*g+s_ref[...].astype(F32)).astype(BF)
    n2_ref[...]=n2
    at=lax.broadcasted_iota(jnp.int32,(8,TB),1)+i*TB
    keep=jnp.where((tg_ref[...]>=0)&(at<live),1.0,0.0)
    keep=keep.T[:,0:1]
    top=og_ref[...].astype(F32)*keep
    dl=top.astype(BF)
    dl_ref[...]=dl
    sum_ref[3:4,:]+=jnp.sum(top,axis=0,keepdims=True)
    first=True
    for wu,bu,wd,a_ref,u_ref,sb in ((wuo_ref,buo_ref,wdo_ref,ao_ref,uo_ref,sbo_ref),(wup_ref,bup_ref,wdp_ref,ap_ref,up_ref,sbp_ref)):
        for c in range(0,wu.shape[1],FC):
            h=nn(n2,wu[:,c:c+FC])+bu[:,c:c+FC].astype(F32)
            ag=nt(dl,wd[c:c+FC,:])
            val,slope=gelu_parts(h)
            a=val.astype(BF)
            hg=ag*slope
            u=hg.astype(BF)
            a_ref[:,c:c+FC]=a; u_ref[:,c:c+FC]=u
            sb[0:1,c:c+FC]+=jnp.sum(hg,axis=0,keepdims=True)
    feed=nn(ao_ref[...],wdo_ref[...])+nn(ap_ref[...],wdp_ref[...])
    out_ref[...]=(mid+feed+bd_ref[...].astype(F32)).astype(BF)
    sg=nt(uo_ref[...],wuo_ref[...])+nt(up_ref[...],wup_ref[...])
    sum_ref[0:1,:]+=jnp.sum(sg*nrm,axis=0,keepdims=True)
    sum_ref[1:2,:]+=jnp.sum(sg,axis=0,keepdims=True)
    inner=sg*g
    mg=top+r*(inner-jnp.mean(inner,axis=-1,keepdims=True)-nrm*jnp.mean(inner*nrm,axis=-1,keepdims=True))
    mg_ref[...]=mg
    sum_ref[2:3,:]+=jnp.sum(mg,axis=0,keepdims=True)
    bl=mg.astype(BF)
    bl_ref[...]=bl
    xg_ref[...]=nt(bl,wo[...]).astype(BF)

def ffn_call(meta,mixed,x,og,targets,wo_own,wo_par,b_out,g,s,wu_own,wu_par,bu_own,bu_par,wd_own,wd_par,b_down):
    T,D=x.shape; inner=mixed.shape[1]; fh=wu_own.shape[1]
    rows=lambda n:pl.BlockSpec((TB,n),lambda i,m:(i,0))
    one=full((1,D))
    return pl.pallas_call(ffn_kernel,
        out_shape=(sd((T,D),BF),sd((T,D),BF),sd((T,fh),BF),sd((T,fh),BF),sd((T,fh),BF),sd((T,fh),BF),sd((T,D),BF),sd((T,D),F32),sd((T,D),BF),sd((T,inner),BF),
                   sd((8,D),F32),sd((8,fh),F32),sd((8,fh),F32)),
        grid_spec=pltpu.PrefetchScalarGridSpec(num_scalar_prefetch=1,grid=(T//TB,),
            in_specs=[rows(inner),rows(D),rows(D),pl.BlockSpec((1,TB),lambda i,m:(0,i)),full(wo_own.shape),full(wo_par.shape),one,one,one,
                      full(wu_own.shape),full(wu_par.shape),full((1,fh)),full((1,fh)),full(wd_own.shape),full(wd_par.shape),one],
            out_specs=(rows(D),rows(D),rows(fh),rows(fh),rows(fh),rows(fh),rows(D),rows(D),rows(D),rows(inner),full((8,D)),full((8,fh)),full((8,fh))),
            scratch_shapes=[pltpu.VMEM((inner,D),BF),pltpu.VMEM((TB,D),F32),pltpu.VMEM((TB,D),F32)]),
        compiler_params=params(56),
        cost_estimate=pl.CostEstimate(flops=2*T*D*(2*inner+8*fh),bytes_accessed=30<<20,transcendentals=0),
        name="mix_ffn_both_ways")(meta,mixed,x,og,targets,wo_own,wo_par,b_out,g,s,wu_own,wu_par,bu_own,bu_par,wd_own,wd_par,b_down)

def ffn_grads_kernel(n_ref,dl_ref,mix_ref,bl_ref,ao_ref,ap_ref,uo_ref,up_ref,guo_ref,gup_ref,gdo_ref,gdp_ref,goo_ref,gop_ref,nT):
    i=pl.program_id(0)
    @pl.when(i==0)
    def _():
        nT[...]=n_ref[...].T
        go=tn(mix_ref[...],bl_ref[...]).astype(BF)
        h=goo_ref.shape[0]
        goo_ref[...]=go[0:h]; gop_ref[...]=go[h:2*h]
    guo_ref[...]=nn(nT[...],uo_ref[...]).astype(BF)
    gup_ref[...]=nn(nT[...],up_ref[...]).astype(BF)
    gdo_ref[...]=tn(ao_ref[...],dl_ref[...]).astype(BF)
    gdp_ref[...]=tn(ap_ref[...],dl_ref[...]).astype(BF)

def ffn_grads_call(n2,dl,mixed,bl,ao,ap,uo,up):
    T,D=n2.shape; fh=ao.shape[1]; inner=mixed.shape[1]
    cols=pl.BlockSpec((T,FC),lambda i:(0,i))
    wide=pl.BlockSpec((D,FC),lambda i:(0,i)); tall=pl.BlockSpec((FC,D),lambda i:(i,0))
    return pl.pallas_call(ffn_grads_kernel,
        out_shape=(sd((D,fh),BF),sd((D,fh),BF),sd((fh,D),BF),sd((fh,D),BF),sd((inner//2,D),BF),sd((inner//2,D),BF)),
        grid=(fh//FC,),
        in_specs=[full((T,D)),full((T,D)),full((T,inner)),full((T,D)),cols,cols,cols,cols],
        out_specs=(wide,wide,tall,tall,full((inner//2,D)),full((inner//2,D))),
        scratch_shapes=[pltpu.VMEM((D,T),BF)],
        compiler_params=params(48),
        cost_estimate=pl.CostEstimate(flops=2*T*D*(4*fh+inner),bytes_accessed=24<<20,transcendentals=0),
        name="ffn_weight_grads")(n2,dl,mixed,bl,ao,ap,uo,up)

def in_grad_kernel(dq_ref,dk_ref,dv_ref,w_ref,x_ref,mg_ref,g_ref,out_ref,sum_ref):
    i=pl.program_id(0)
    @pl.when(i==0)
    def _():
        sum_ref[...]=jnp.zeros_like(sum_ref)
    fg=nt(dq_ref[...],w_ref[0])+nt(dk_ref[...],w_ref[1])+nt(dv_ref[...],w_ref[2])
    nrm,r=ln_stats(x_ref[...].astype(F32))
    sum_ref[0:1,:]+=jnp.sum(fg*nrm,axis=0,keepdims=True)
    sum_ref[1:2,:]+=jnp.sum(fg,axis=0,keepdims=True)
    inner=fg*g_ref[...].astype(F32)
    out_ref[...]=(mg_ref[...]+r*(inner-jnp.mean(inner,axis=-1,keepdims=True)-nrm*jnp.mean(inner*nrm,axis=-1,keepdims=True))).astype(BF)

def in_grad_call(dq,dk,dv,wc,x,mg,g):
    T,D=x.shape; inner=dq.shape[1]
    rows=lambda n:pl.BlockSpec((TB,n),lambda i:(i,0))
    return pl.pallas_call(in_grad_kernel,
        out_shape=(sd((T,D),BF),sd((8,D),F32)),grid=(T//TB,),
        in_specs=[rows(inner)]*3+[full(wc.shape),rows(D),rows(D),full((1,D))],
        out_specs=(rows(D),full((8,D))),
        compiler_params=params(40),
        cost_estimate=pl.CostEstimate(flops=6*T*D*inner,bytes_accessed=14<<20,transcendentals=0),
        name="input_grad")(dq,dk,dv,wc,x,mg,g)

def qkv_grads_kernel(n_ref,dq_ref,dk_ref,dv_ref,own_ref,par_ref):
    nT=n_ref[...].T
    half=own_ref.shape[2]
    for c,r in enumerate((dq_ref,dk_ref,dv_ref)):
        g=nn(nT,r[...]).astype(BF)
        own_ref[c]=g[:,0:half]; par_ref[c]=g[:,half:2*half]

def qkv_grads_call(n1,dq,dk,dv):
    T,D=n1.shape; inner=dq.shape[1]
    return pl.pallas_call(qkv_grads_kernel,
        out_shape=(sd((3,D,inner//2),BF),)*2,
        compiler_params=params(48),
        in_specs=[pl.BlockSpec(memory_space=pltpu.VMEM)]*4,out_specs=(pl.BlockSpec(memory_space=pltpu.VMEM),)*2,
        cost_estimate=pl.CostEstimate(flops=6*T*D*inner,bytes_accessed=8<<20,transcendentals=0),
        name="qkv_weight_grads")(n1,dq,dk,dv)


def swap_cores(a):
    return lax.ppermute(a,"tensor",[(0,1),(1,0)])

def sum_everywhere(a):
    n=lax.axis_size("dp")
    a=a+swap_cores(a)
    step=1
    while step<n:
        a=a+lax.ppermute(a,"dp",[(i,i^step) for i in range(n)])
        step*=2
    return a

def body(tokens,out_grad,segment_ids,token_live,live_rows,targets,predicted,w_qkv,b_qkv,w_out,b_out,
         norm1_gain,norm1_bias,norm2_gain,norm2_bias,w_up,b_up,w_down,b_down):
    member=lax.axis_index("tensor")
    x=tokens[0]; T,D=x.shape
    half=w_qkv.shape[2]; fh=w_up.shape[1]
    w_qkv_p=swap_cores(w_qkv)
    bias_own=jnp.concatenate([b_qkv.reshape(1,3*half),b_up.reshape(1,fh)],axis=1)
    bias_par=swap_cores(bias_own)
    w_out_p=swap_cores(w_out); w_up_p=swap_cores(w_up); w_down_p=swap_cores(w_down)
    segments=lax.dynamic_index_in_dim(segment_ids,member,0,keepdims=False)
    lived=lax.dynamic_index_in_dim(token_live,member,0,keepdims=False)
    starts=jnp.sum((segments[None,:]<jnp.arange(9,dtype=jnp.int32)[:,None]).astype(jnp.int32),axis=1)
    live=jnp.where(member<live_rows[0],jnp.sum(lived),0)
    meta=jnp.concatenate([starts,live[None],jnp.zeros((6,),jnp.int32)])
    row=lambda a:a.reshape(1,-1)
    b_cat=jnp.concatenate([bias_own[:,:3*half].reshape(3,half),bias_par[:,:3*half].reshape(3,half)],axis=1).astype(F32)
    g1,s1,g2,s2=row(norm1_gain),row(norm1_bias),row(norm2_gain),row(norm2_bias)
    n1,q,k,v,cos,sin,wc=qkv_call(meta,x,w_qkv,w_qkv_p,b_cat,g1,s1)
    mixed,lse=attend_fwd(meta,q,k,v)
    n2,dl,ao,ap,uo,up,out_act,mg,bl,xg,sums,sbo,sbp=ffn_call(meta,mixed,x,out_grad[0],targets,w_out,w_out_p,row(b_out),g2,s2,
        w_up,w_up_p,bias_own[:,3*half:],bias_par[:,3*half:],w_down,w_down_p,row(b_down))
    guo,gup,gdo,gdp,goo,gop=ffn_grads_call(n2,dl,mixed,bl,ao,ap,uo,up)
    join=lambda o,p:(o.astype(F32)+swap_cores(p).astype(F32)).astype(BF)
    ffn=lax.psum((join(guo,gup),join(gdo,gdp),join(goo,gop)),"dp")
    dq,dk,dv,psum3=attend_bwd(meta,q,k,v,mixed,xg,lse,cos,sin)
    in_grad,sums1=in_grad_call(dq,dk,dv,wc,x,mg,g1)
    gqo,gqp=qkv_grads_call(n1,dq,dk,dv)
    gqkv=lax.psum(join(gqo,gqp),"dp")
    masked=(targets[0]>=0)&(jnp.arange(T)<live)
    correct=masked&(predicted[0]==targets[0])
    row_correct=jnp.sum(correct.astype(jnp.int32))[None]
    tallies=jnp.stack([live.astype(F32),jnp.sum(masked.astype(F32)),row_correct[0].astype(F32)])
    bq=psum3[:,0:3,:].transpose(1,0,2).reshape(3,2*half)
    own=jnp.concatenate([bq[:,:half].reshape(-1),sbo[0]]); par=jnp.concatenate([bq[:,half:].reshape(-1),sbp[0]])
    shared=jnp.concatenate([sums[2],sums[3],sums1[0],sums1[1],sums[0],sums[1],tallies,jnp.zeros((-(3*half+fh+6*D+3)%TILE,),F32)])
    small=jnp.concatenate([own,shared]).reshape(-1,TILE)
    other=jnp.concatenate([par,shared]).reshape(-1,TILE)
    small=small+swap_cores(other)
    n=lax.axis_size("dp"); step=1
    while step<n:
        small=small+lax.ppermute(small,"dp",[(i,i^step) for i in range(n)])
        step*=2
    small=small.reshape(-1)
    base=3*half+fh
    totals=small[base+6*D:base+6*D+3]
    factor=n/totals[1]
    part=lambda i:small[base+i*D:base+(i+1)*D]*factor
    return (out_act[None],in_grad[None],gqkv.astype(F32)*factor,small[:3*half].reshape(3,half)*factor,ffn[2].astype(F32)*factor,part(0),
            part(2),part(3),part(4),part(5),ffn[0].astype(F32)*factor,small[3*half:base]*factor,ffn[1].astype(F32)*factor,part(1),
            totals.astype(jnp.int32),row_correct)


def solution(mesh):
    in_specs = (
        P(("dp", "tensor"), None, None),
        P(("dp", "tensor"), None, None),
        P("dp", None),
        P("dp", None),
        P("dp"),
        P(("dp", "tensor"), None),
        P(("dp", "tensor"), None),
        P(None, None, "tensor"),
        P(None, "tensor"),
        P("tensor", None),
        P(),
        P(),
        P(),
        P(),
        P(),
        P(None, "tensor"),
        P("tensor"),
        P("tensor", None),
        P(),
    )
    out_specs = (
        P(("dp", "tensor"), None, None),
        P(("dp", "tensor"), None, None),
        P(None, None, "tensor"),
        P(None, "tensor"),
        P("tensor", None),
        P(),
        P(),
        P(),
        P(),
        P(),
        P(None, "tensor"),
        P("tensor"),
        P("tensor", None),
        P(),
        P(),
        P(("dp", "tensor")),
    )
    return jax.shard_map(body, mesh=mesh, in_specs=in_specs, out_specs=out_specs, check_vma=False)
```

time: 869 us -> 425 us (0.49)
  matrix products: 266 us -> 0 us
  Pallas kernels: 0 us -> 163 us
  other arithmetic: 148 us -> 20.1 us
  blocking collectives: 121 us -> 0 us
  waiting for transfers between devices: 227 us -> 165 us
  local copies, waits for them, and re-layouts: 82 us -> 38.9 us
  starting transfers between devices: 1.01 us -> 12.7 us
    dot_general x40 -> x0, matrix products: 266 us -> none  [the longest x4 57.5 us: attend_backward(): jnp.einsum('qhe,khe->hqk', block_grad, value_heads, preferred_element_typ...]
    pallas_call x0 -> x7, Pallas kernels: none -> 163 us  [the longest x1 67 us: attend_bwd(): pl.pallas_call(bwd_kernel, out_shape=(sd((length, cols), BF),) * 3 + (sd(...]
    psum x2 -> x0, blocking collectives: 121 us -> none  [the longest x1 82.1 us: body(): lax.psum((grad_w_qkv, grad_b_qkv, grad_w_out, grad_w_up, grad_b_up, grad_...]
    convert_element_type x22 -> x6, other arithmetic: 70.2 us -> 9.22 us  [the longest x4 8.56 us: body(): join = lambda o, p: (o.astype(F32) + swap_cores(p).astype(F32)).astype(BF)]
    while x60 -> x0, local copies, waits for them, and re-layouts: 55.5 us -> none
    reduce_sum x15 -> x4, other arithmetic: 45.5 us -> 2.73 us  [the longest x1 1.36 us: body(): live = jnp.where(member < live_rows[0], jnp.sum(lived), 0)]
    all_gather x4 -> x0, waiting for transfers between devices: 37.3 us -> none  [the longest x1 12.7 us: body(): lax.all_gather(middle_grad.astype(jnp.bfloat16), 'tensor', axis=0, tiled=...]
    reduce_scatter x4 -> x0, waiting for transfers between devices: 28.5 us -> none  [the longest x1 13.9 us: body(): lax.psum_scatter(jnp.einsum('rle,ed->rld', picked, w_out_use, preferred_e...]
  transfers between devices with their start and end apart: 9 -> 15, of which waited for: 8 -> 6; matrix products, arithmetic and copies ran while one was open for 8% -> 8% of each run, Pallas kernels for 0% -> 29%
where the time goes in v1:
time: 425 us; the launch traced here: 417 us
  waiting for transfers between devices  165 us (39%)
  Pallas kernels  163 us (38%)
  local copies, waits for them, and re-layouts  38.9 us (9%)
  other arithmetic  20.1 us (5%)
  between operations  17.5 us (4%)
  starting transfers between devices  12.7 us (3%)
    psum x1, waiting for transfers between devices, body(): gqkv = lax.psum(join(gqo, gqp), 'dp')  149 us
    pallas_call x1, Pallas kernels, attend_bwd(): pl.pallas_call(bwd_kernel, out_shape=(sd((length, cols), BF),) * 3 + (sd(...  67 us
    pallas_call x1, Pallas kernels, attend_fwd(): pl.pallas_call(fwd_kernel, out_shape=(jax.ShapeDtypeStruct((length, cols)...  32.8 us
    pallas_call x1, Pallas kernels, ffn_call(): pl.pallas_call(ffn_kernel, out_shape=(sd((T, D), BF), sd((T, D), BF), sd(...  31 us
    unnamed x88, local copies, waits for them, and re-layouts  20 us
    ppermute x4, waiting for transfers between devices, body(): small = small + lax.ppermute(small, 'dp', [(i, i ^ step) for i in range(n)])  12.6 us
    pallas_call x1, Pallas kernels, ffn_grads_call(): pl.pallas_call(ffn_grads_kernel, out_shape=(sd((D, fh), BF), sd((D, fh),...  12.1 us
    ppermute x4, starting transfers between devices, body(): small = small + lax.ppermute(small, 'dp', [(i, i ^ step) for i in range(n)])  9.45 us
  transfers between devices with their start and end apart: 15, of which 6 were waited for; matrix products, arithmetic and copies ran while one was open for 8% of the time, Pallas kernels for 29%

profile of v1, /device:TPU:0, one launch (start us, length us, event | category | flops | bytes accessed | tf_op | source)
XLA Modules:
  0.0 417.4 jit_solution(11956880392581008562)
XLA Ops:
  7.3 0.5 collective-permute-start
  7.9 0.4 collective-permute-start.4
  8.3 0.7 reshape.86.buo_ref
  9.0 0.8 reshape.85
  11.0 1.4 dynamic-slice_reduce_fusion
  13.3 2.5 copy.45.wo_ref
  15.9 0.6 reshape.90.bo_ref
  16.5 0.6 reshape.91.g_ref
  17.1 0.6 reshape.92.s_ref
  17.7 0.6 reshape.93.bd_ref
  18.3 0.7 slice.94.bup_ref
  19.1 3.5 copy.46.wp_ref
  22.6 1.0 copy-done.13
  23.6 9.3 %norm_qkv_rope.1 = (bf16[1024,640]{1,0:T(8,128)(2,1)S(1)}, bf16[1024,640]{1,0:T(8,128)(2,1)S(1)}, bf16[1024,640]{1,0:T(8,128)(2,1)S(1)}, bf16[1024,640]{1,0:T(8,...) custom-call(s32[16]{0:T(128)S(1)} %pad_add_fusion.meta, ...), custom_call_target="tpu_custom_call" | custom-call | flops 2516582400 | bytes 12582912 | tf_op jit(solution)/shard_map/norm_qkv_rope/pallas_call | solution.py:239
  32.9 0.8 copy-done.19
  33.7 32.8 %attend_fwd.1 = (bf16[1024,640]{1,0:T(8,128)(2,1)S(1)}, f32[5,4,1024]{2,1,0:T(4,128)S(1)}) custom-call(s32[16]{0:T(128)S(1)} %pad_add_fusion.meta, bf16[1024,640]{1,0:T(8,128)(2,1)S(1)} %get-tuple-element.52.q_ref, bf16[1024,640]{1,0:T(8,128)(2,1)S(1)} %get-tuple-element.53.k_ref, bf16[1024,640]{1,0:T(8,128)(2,1)S(1)} %get-tuple-element.54.v_ref), custom_call_target="tpu_custom_call" | custom-call | flops 2684354560 | bytes 6291456 | tf_op jit(solution)/shard_map/attend_fwd/pallas_call | solution.py:94
  66.6 1.0 copy-done.17
  67.6 31.0 %mix_ffn_both_ways.1 = (bf16[1024,640]{1,0:T(8,128)(2,1)}, bf16[1024,640]{1,0:T(8,128)(2,1)}, bf16[1024,1280]{1,0:T(8,128)(2,1)}, bf16[1024,1280]{1,0:T(8,128)(2...) custom-call(s32[16]{0:T(128)} %copy-done.10, ...), custom_call_target="tpu_custom_call" | custom-call | flops 15099494400 | bytes 31457280 | tf_op jit(solution)/shard_map/mix_ffn_both_ways/pallas_call | solution.py:301
  98.7 1.3 copy-done.23
  100.0 1.3 copy-done.24
  101.3 1.3 copy-done.25
  102.6 12.1 %ffn_weight_grads.1 = (bf16[640,1280]{1,0:T(8,128)(2,1)}, bf16[640,1280]{1,0:T(8,128)(2,1)}, bf16[1280,640]{1,0:T(8,128)(2,1)}, bf16[1280,640]{1,0:T(8,128)(2,1)...) custom-call(bf16[1024,640]{1,0:T(8,128)(2,1)S(1)} %copy-done.23, bf16[1024,640]{1,0:T(8,128)(2,1)S(1)} %copy-done.24, ...), custom_call_target="tpu_custom_call" | custom-call | flops 7549747200 | bytes 25165824 | tf_op jit(solution)/shard_map/ffn_weight_grads/pallas_call | solution.py:330
  114.7 0.6 collective-permute-start.13
  115.4 67.0 %attend_bwd.1 = (bf16[1024,640]{1,0:T(8,128)(2,1)S(1)}, bf16[1024,640]{1,0:T(8,128)(2,1)S(1)}, bf16[1024,640]{1,0:T(8,128)(2,1)S(1)}, f32[5,8,128]{2,1,0:T(8,128)S(1)}) custom-call(s32[16]{0:T(128)S(1)} %copy-done.11, bf16[1024,640]{1,0:T(8,128)(2,1)} %copy-done.14, bf16[1024,640]{1,0:T(8,128)(2,1)} %copy-done.15, bf16[1024,640]{1,0:T(8,128)(2,1)} %copy-done.16, ...), custom_call_target="tpu_custom_call" | custom-call | flops 6710886400 | bytes 10485760 | tf_op jit(solution)/shard_map/attend_bwd/pallas_call | solution.py:169
  182.4 4.9 %qkv_weight_grads.1 = (bf16[3,640,320]{2,1,0:T(8,128)(2,1)}, bf16[3,640,320]{2,1,0:T(8,128)(2,1)}) custom-call(bf16[1024,640]{1,0:T(8,128)(2,1)S(1)} %get-tuple-element.67.n_ref, bf16[1024,640]{1,0:T(8,128)(2,1)S(1)} %get-tuple-element.61.dq_ref, bf16[1024,640]{1,0:T(8,128)(2,1)S(1)} %get-tuple-element.62.dk_ref, bf16[1024,640]{1,0:T(8,128)(2,1)S(1)} %get-tuple-element.63.dv_ref), custom_call_target="tpu_custom_call" | custom-call | flops 2516582400 | bytes 8388608 | tf_op jit(solution)/shard_map/qkv_weight_grads/pallas_call | solution.py:372
  187.3 3.5 copy.47
  190.8 0.5 collective-permute-start.11
  191.3 3.2 collective-permute-done.11
  194.5 0.9 add_convert_fusion.3
  195.4 2.6 copy.48
  198.1 1.5 add_convert_fusion.2
  199.8 3.2 add_convert_fusion
  202.9 3.1 add_convert_fusion.1
  206.0 0.7 copy-done.35
  206.7 0.6 convert_reduce_fusion.1
  208.0 0.6 convert_reduce_fusion.2
  208.8 1.7 copy-done.1
  210.5 1.3 copy-done.3
  211.8 1.3 copy-done.5
  213.1 1.3 copy-done.7
  214.4 1.4 copy-done.9
  215.9 6.0 %input_grad.1 = (bf16[1024,640]{1,0:T(8,128)(2,1)}, f32[8,640]{1,0:T(8,128)S(1)}) custom-call(bf16[1024,640]{1,0:T(8,128)(2,1)S(1)} %copy-done.5, bf16[1024,640]{1,0:T(8,128)(2,1)S(1)} %copy-done.7, bf16[1024,640]{1,0:T(8,128)(2,1)S(1)} %copy-done.9, bf16[3,640,640]{2,1,0:T(8,128)(2,1)S(1)} %copy-done.1, bf16[1024,640]{1,0:T(8,128)(2,1)S(1)} %bitcast.26, ...), custom_call_target="tpu_custom_call" | custom-call | flops 2516582400 | bytes 14680064 | tf_op jit(solution)/shard_map/input_grad/pallas_call | solution.py:355
  221.9 0.8 slice_reduce_fusion
  222.8 0.7 concatenate.22
  223.5 0.5 collective-permute-start.6
  224.0 0.8 slice_reduce_fusion.1
  224.9 0.7 concatenate.21
  225.7 4.3 %collective-permute-done.7 = f32[48,128]{1,0:T(8,128)S(1)} collective-permute-done((f32[48,128]{1,0:T(8,128)S(1)}, f32[48,128]{1,0:T(8,128)S(1)}, u32[]{:S(2)}, u32[]{:S(2)}) %collective-permute-start.7) | collective-permute-done | bytes 24608 | tf_op jit(solution)/shard_map/ppermute | solution.py:432
  230.0 2.0 collective-permute-start.8
  232.0 1.8 collective-permute-done.8
  233.9 1.8 collective-permute-start.9
  235.7 2.9 collective-permute-done.9
  238.6 5.6 %collective-permute-start.10 = (f32[48,128]{1,0:T(8,128)S(1)}, f32[48,128]{1,0:T(8,128)S(1)}, u32[]{:S(2)}, u32[]{:S(2)}) collective-permute-start(f32[48,128]{1,0:T(8,128)S(1)} %add.45), channel_id=1, source_target_pairs={{0,16},{2,18},{4,20},{6,22},{8,24},{10,26},{12,28},{14,30},{16,0},... | collective-permute-start | bytes 73736 | tf_op jit(solution)/shard_map/ppermute | solution.py:432
  244.1 3.6 collective-permute-done.10
  247.8 0.6 slice.97
  249.0 0.7 mul.69
  249.7 0.6 slice_convert_fusion
  250.3 0.7 slice_multiply_fusion
  251.0 0.7 slice_multiply_fusion.1
  251.7 149.4 %all-reduce.3.cloned.1.call-done = (bf16[3,640,320]{2,1,0:T(8,128)(2,1)}, bf16[320,640]{1,0:T(8,128)(2,1)}, bf16[640,1280]{1,0:T(8,128)(2,1)}, bf16[1280,640]{1,0:T(8,128)(2,1)}) async-done(((bf16[3,640,320]{2,1,0:T(8,128)(2,1)}, bf16[320,640]{1,0:T(8,128)(2,1)}, bf16[640,1280]{1,0:T(8,128)(2,1)}, bf16[1280,640]{1,0:T(8,128)(2,1)}), (bf16[3,640,320]{2,1,0:T(8,128)(2,1)}, bf16[320,640]{1,0:T(8,128)(2,1)}, ...) | async-done | bytes 4915216 | tf_op jit(solution)/shard_map/psum | solution.py:419
  401.0 3.5 convert_multiply_fusion
  404.5 1.9 convert_multiply_fusion.1
  406.5 0.9 convert_multiply_fusion.3
  407.6 2.6 copy.49
  (115 shorter events, 2.2 us)
Async XLA Ops:
  7.2 11.8 %copy-start.33 = (bf16[3,320]{1,0:T(4,128)(2,1)S(1)}, bf16[3,320]{1,0:T(4,128)(2,1)}, u32[]{:S(2)}) copy-start(bf16[3,320]{1,0:T(4,128)(2,1)} %param.29) | copy-start | bytes 5764
  7.2 8.6 %copy-start.37 = (bf16[640]{0:T(1024)(128)(2,1)S(1)}, bf16[640]{0:T(1024)(128)(2,1)}, u32[]{:S(2)}) copy-start(bf16[640]{0:T(1024)(128)(2,1)} %param.32) | copy-start | bytes 3844
  7.2 8.7 %copy-start.38 = (bf16[640]{0:T(1024)(128)(2,1)S(1)}, bf16[640]{0:T(1024)(128)(2,1)}, u32[]{:S(2)}) copy-start(bf16[640]{0:T(1024)(128)(2,1)} %param.33) | copy-start | bytes 3844
  7.2 8.7 %copy-start.39 = (bf16[640]{0:T(1024)(128)(2,1)S(1)}, bf16[640]{0:T(1024)(128)(2,1)}, u32[]{:S(2)}) copy-start(bf16[640]{0:T(1024)(128)(2,1)} %param.31) | copy-start | bytes 3844
  7.2 9.3 %copy-start.40 = (bf16[640]{0:T(1024)(128)(2,1)S(1)}, bf16[640]{0:T(1024)(128)(2,1)}, u32[]{:S(2)}) copy-start(bf16[640]{0:T(1024)(128)(2,1)} %param.34) | copy-start | bytes 3844
  7.2 9.8 %copy-start.41 = (bf16[640]{0:T(1024)(128)(2,1)S(1)}, bf16[640]{0:T(1024)(128)(2,1)}, u32[]{:S(2)}) copy-start(bf16[640]{0:T(1024)(128)(2,1)} %param.35) | copy-start | bytes 3844
  7.2 10.4 %copy-start.42 = (bf16[640]{0:T(1024)(128)(2,1)S(1)}, bf16[640]{0:T(1024)(128)(2,1)}, u32[]{:S(2)}) copy-start(bf16[640]{0:T(1024)(128)(2,1)} %param.39) | copy-start | bytes 3844
  7.3 393.8 %all-reduce.3.cloned.1.call-start = ((), (), s32[]{:S(2)}) async-start(), calls=%async_computation | async-start | bytes 10321920 | tf_op jit(solution)/shard_map/psum | solution.py:419
  7.3 11.8 %collective-permute-start = (bf16[3,640,320]{1,2,0:T(8,128)(2,1)}, bf16[3,640,320]{1,2,0:T(8,128)(2,1)}, u32[]{:S(2)}, u32[]{:S(2)}) collective-permute-start(bf16[3,640,320]{1,2,0:T(8,128)(2,1)} %param.28), channel_id=1, source_target_pairs={{0,1},{1,0},{2,3},{3,2},{4,5},{5,4},{6,7},{7,6},{8,9},{9,8},{10,11... | collective-permute-start | bytes 3686408 | tf_op jit(solution)/shard_map/ppermute | solution.py:381
  7.8 59.8 %collective-permute-start.3 = (bf16[640,1280]{1,0:T(8,128)(2,1)}, bf16[640,1280]{1,0:T(8,128)(2,1)}, u32[]{:S(2)}, u32[]{:S(2)}) collective-permute-start(bf16[640,1280]{1,0:T(8,128)(2,1)} %wuo_ref.1), channel_id=1, source_target_pairs={{0,1},{1,0},{2,3},{3,2},{4,5},{5,4},{6,7},{7,6},{8,9},{9,8},{10,11... | collective-permute-start | bytes 4915208 | tf_op jit(solution)/shard_map/ppermute | solution.py:381
  7.9 59.7 %collective-permute-start.4 = (bf16[1280,640]{1,0:T(8,128)(2,1)}, bf16[1280,640]{1,0:T(8,128)(2,1)}, u32[]{:S(2)}, u32[]{:S(2)}) collective-permute-start(bf16[1280,640]{1,0:T(8,128)(2,1)} %wdo_ref.1), channel_id=1, source_target_pairs={{0,1},{1,0},{2,3},{3,2},{4,5},{5,4},{6,7},{7,6},{8,9},{9,8},{10,11... | collective-permute-start | bytes 4915208 | tf_op jit(solution)/shard_map/ppermute | solution.py:381
  9.0 13.6 %copy-start.32 = (bf16[1,1280]{1,0:T(2,128)(2,1)}, bf16[1,1280]{1,0:T(2,128)(2,1)S(1)}, u32[]{:S(2)}) copy-start(bf16[1,1280]{1,0:T(2,128)(2,1)S(1)} %reshape.86.buo_ref) | copy-start | bytes 7684
  9.9 8.4 %collective-permute-start.1 = (bf16[1,2240]{1,0:T(2,128)(2,1)S(1)}, bf16[1,2240]{1,0:T(2,128)(2,1)S(1)}, u32[]{:S(2)}, u32[]{:S(2)}) collective-permute-start(bf16[1,2240]{1,0:T(2,128)(2,1)S(1)} %pad_maximum_fusion), channel_id=1, source_target_pairs={{0,1},{1,0},{2,3},{3,2},{4,5},{5,4},{6,7},{7,6},{8,9},{9,8},{10,11... | collective-permute-start | bytes 13448 | tf_op jit(solution)/shard_map/ppermute | solution.py:381
  10.0 57.7 %collective-permute-start.2 = (bf16[320,640]{1,0:T(8,128)(2,1)}, bf16[320,640]{1,0:T(8,128)(2,1)}, u32[]{:S(2)}, u32[]{:S(2)}) collective-permute-start(bf16[320,640]{1,0:T(8,128)(2,1)} %woo_ref.1), channel_id=1, source_target_pairs={{0,1},{1,0},{2,3},{3,2},{4,5},{5,4},{6,7},{7,6},{8,9},{9,8},{10,11... | collective-permute-start | bytes 1228808 | tf_op jit(solution)/shard_map/ppermute | solution.py:381
  13.3 20.5 %copy-start.10 = (s32[16]{0:T(128)}, s32[16]{0:T(128)S(1)}, u32[]{:S(2)}) copy-start(s32[16]{0:T(128)S(1)} %pad_add_fusion.meta) | copy-start | bytes 196
  15.8 6.8 %copy-start.2 = (bf16[1,1024,640]{2,1,0:T(8,128)(2,1)S(1)}, bf16[1,1024,640]{2,1,0:T(8,128)(2,1)}, u32[]{:S(2)}) copy-start(bf16[1,1024,640]{2,1,0:T(8,128)(2,1)} %param.21) | copy-start | bytes 3932164
  15.8 6.8 %copy-start.12 = (f32[1024,128]{1,0:T(8,128)S(1)}, f32[1024,128]{1,0:T(8,128)}, u32[]{:S(2)}) copy-start(f32[1024,128]{1,0:T(8,128)} %constant.25.clone.ct_ref) | copy-start | bytes 1572868
  22.6 1.0 copy-start.13
  32.9 0.8 copy-start.19
  33.7 32.8 %copy-start.14 = (bf16[1024,640]{1,0:T(8,128)(2,1)}, bf16[1024,640]{1,0:T(8,128)(2,1)S(1)}, u32[]{:S(2)}) copy-start(bf16[1024,640]{1,0:T(8,128)(2,1)S(1)} %get-tuple-element.52.q_ref) | copy-start | bytes 3932164
  33.7 32.8 %copy-start.15 = (bf16[1024,640]{1,0:T(8,128)(2,1)}, bf16[1024,640]{1,0:T(8,128)(2,1)S(1)}, u32[]{:S(2)}) copy-start(bf16[1024,640]{1,0:T(8,128)(2,1)S(1)} %get-tuple-element.53.k_ref) | copy-start | bytes 3932164
  33.7 32.8 %copy-start.16 = (bf16[1024,640]{1,0:T(8,128)(2,1)}, bf16[1024,640]{1,0:T(8,128)(2,1)S(1)}, u32[]{:S(2)}) copy-start(bf16[1024,640]{1,0:T(8,128)(2,1)S(1)} %get-tuple-element.54.v_ref) | copy-start | bytes 3932164
  33.7 32.8 %copy-start.21 = (f32[1024,128]{1,0:T(8,128)}, f32[1024,128]{1,0:T(8,128)S(1)}, u32[]{:S(2)}) copy-start(f32[1024,128]{1,0:T(8,128)S(1)} %get-tuple-element.60.sin_ref) | copy-start | bytes 1572868
  66.6 1.1 copy-start.17
  67.6 31.0 %copy-start.18 = (bf16[1024,640]{1,0:T(8,128)(2,1)S(1)}, bf16[1024,640]{1,0:T(8,128)(2,1)}, u32[]{:S(2)}) copy-start(bf16[1024,640]{1,0:T(8,128)(2,1)} %copy-done.17) | copy-start | bytes 3932164
  98.7 1.3 copy-start.23
  100.0 1.3 copy-start.24
  101.3 1.3 copy-start.25
  102.6 12.7 %copy-start.11 = (s32[16]{0:T(128)S(1)}, s32[16]{0:T(128)}, u32[]{:S(2)}) copy-start(s32[16]{0:T(128)} %copy-done.10) | copy-start | bytes 196
  102.6 12.7 %copy-start.20 = (f32[1024,128]{1,0:T(8,128)S(1)}, f32[1024,128]{1,0:T(8,128)}, u32[]{:S(2)}) copy-start(f32[1024,128]{1,0:T(8,128)} %copy-done.19) | copy-start | bytes 1572868
  102.6 12.7 %copy-start.22 = (f32[1024,128]{1,0:T(8,128)S(1)}, f32[1024,128]{1,0:T(8,128)}, u32[]{:S(2)}) copy-start(f32[1024,128]{1,0:T(8,128)} %copy-done.21) | copy-start | bytes 1572868
  114.7 84.8 %collective-permute-start.13 = (bf16[1280,640]{1,0:T(8,128)(2,1)}, bf16[1280,640]{1,0:T(8,128)(2,1)}, u32[]{:S(2)}, u32[]{:S(2)}) collective-permute-start(bf16[1280,640]{1,0:T(8,128)(2,1)} %get-tuple-element.87), channel_id=1, source_target_pairs={{0,1},{1,0},{2,3},{3,2},{4,5},{5,4},{6,7},{7,6},{8,9},{9,8},{10,11... | collective-permute-start | bytes 4915208 | tf_op jit(solution)/shard_map/ppermute | solution.py:381
  182.4 4.9 %copy-start.4 = (bf16[1024,640]{1,0:T(8,128)(2,1)}, bf16[1024,640]{1,0:T(8,128)(2,1)S(1)}, u32[]{:S(2)}) copy-start(bf16[1024,640]{1,0:T(8,128)(2,1)S(1)} %get-tuple-element.61.dq_ref) | copy-start | bytes 3932164
  182.4 4.9 %copy-start.6 = (bf16[1024,640]{1,0:T(8,128)(2,1)}, bf16[1024,640]{1,0:T(8,128)(2,1)S(1)}, u32[]{:S(2)}) copy-start(bf16[1024,640]{1,0:T(8,128)(2,1)S(1)} %get-tuple-element.62.dk_ref) | copy-start | bytes 3932164
  182.4 4.9 %copy-start.8 = (bf16[1024,640]{1,0:T(8,128)(2,1)}, bf16[1024,640]{1,0:T(8,128)(2,1)S(1)}, u32[]{:S(2)}) copy-start(bf16[1024,640]{1,0:T(8,128)(2,1)S(1)} %get-tuple-element.63.dv_ref) | copy-start | bytes 3932164
  190.8 4.6 %collective-permute-start.5 = (bf16[3,640,320]{1,2,0:T(8,128)(2,1)}, bf16[3,640,320]{1,2,0:T(8,128)(2,1)}, u32[]{:S(2)}, u32[]{:S(2)}) collective-permute-start(bf16[3,640,320]{1,2,0:T(8,128)(2,1)} %copy.47), channel_id=1, source_target_pairs={{0,1},{1,0},{2,3},{3,2},{4,5},{5,4},{6,7},{7,6},{8,9},{9,8},{10,11... | collective-permute-start | bytes 3686408 | tf_op jit(solution)/shard_map/ppermute | solution.py:381
  190.8 3.7 collective-permute-start.11
  191.3 11.6 %collective-permute-start.12 = (bf16[640,1280]{1,0:T(8,128)(2,1)}, bf16[640,1280]{1,0:T(8,128)(2,1)}, u32[]{:S(2)}, u32[]{:S(2)}) collective-permute-start(bf16[640,1280]{1,0:T(8,128)(2,1)} %get-tuple-element.85), channel_id=1, source_target_pairs={{0,1},{1,0},{2,3},{3,2},{4,5},{5,4},{6,7},{7,6},{8,9},{9,8},{10,11... | collective-permute-start | bytes 4915208 | tf_op jit(solution)/shard_map/ppermute | solution.py:381
  195.4 2.7 copy-start.30
  198.1 1.7 copy-start.28
  199.8 3.2 copy-start.27
  206.0 0.7 copy-start.35
  206.0 0.7 copy-start.36
  206.0 2.8 copy-start
  208.8 1.7 copy-start.1
  210.5 1.3 copy-start.3
  211.8 1.3 copy-start.5
  213.1 1.3 copy-start.7
  214.4 1.4 copy-start.9
  215.9 6.9 %copy-start.34 = (f32[8,640]{1,0:T(8,128)S(1)}, f32[8,640]{1,0:T(8,128)}, u32[]{:S(2)}) copy-start(f32[8,640]{1,0:T(8,128)} %get-tuple-element.72) | copy-start | bytes 61444
  223.5 2.1 collective-permute-start.6
  225.6 4.4 %collective-permute-start.7 = (f32[48,128]{1,0:T(8,128)S(1)}, f32[48,128]{1,0:T(8,128)S(1)}, u32[]{:S(2)}, u32[]{:S(2)}) collective-permute-start(f32[48,128]{1,0:T(8,128)S(1)} %bitcast_add_fusion), channel_id=1, source_target_pairs={{0,2},{2,0},{4,6},{6,4},{8,10},{10,8},{12,14},{14,12},{16,18},{18,... | collective-permute-start | bytes 73736 | tf_op jit(solution)/shard_map/ppermute | solution.py:432
  230.0 3.8 collective-permute-start.8
  233.9 4.7 %collective-permute-start.9 = (f32[48,128]{1,0:T(8,128)S(1)}, f32[48,128]{1,0:T(8,128)S(1)}, u32[]{:S(2)}, u32[]{:S(2)}) collective-permute-start(f32[48,128]{1,0:T(8,128)S(1)} %add.44), channel_id=1, source_target_pairs={{0,8},{2,10},{4,12},{6,14},{8,0},{10,2},{12,4},{14,6},{16,24},{18,... | collective-permute-start | bytes 73736 | tf_op jit(solution)/shard_map/ppermute | solution.py:432
  238.6 9.2 %collective-permute-start.10 = (f32[48,128]{1,0:T(8,128)S(1)}, f32[48,128]{1,0:T(8,128)S(1)}, u32[]{:S(2)}, u32[]{:S(2)}) collective-permute-start(f32[48,128]{1,0:T(8,128)S(1)} %add.45), channel_id=1, source_target_pairs={{0,16},{2,18},{4,20},{6,22},{8,24},{10,26},{12,28},{14,30},{16,0},... | collective-permute-start | bytes 73736 | tf_op jit(solution)/shard_map/ppermute | solution.py:432
  401.0 3.5 copy-start.26
  404.5 1.9 copy-start.31
  404.5 2.9 copy-start.29
Sparse Core Ops, SparseCore 0:
  206.2 194.8 all-reduce.2
